TPU v7x, 256 devices: a whole 4x4x8 slice. The times are simulated.
256 devices in a mesh: grp: 8 (over x, y_hi), blk: 32 (over z, y_lo, core).
Axes of the slice: x: 4, y: 4 (y_hi: 2, y_lo: 2; y = y_hi * 2 + y_lo), z: 8, core: 2. Of those that a mesh axis runs over, the one named last changes fastest.
Arguments:
- counts: int32 [65536, 1024], P(('grp', 'blk')), may hold values from 0 to 5
- tile_live: int32 [512, 8], P(('grp', 'blk')), may hold values from 0 to 1
- doc_lengths: int32 [65536], P(('grp', 'blk')), may hold values from 256 to 4095
- doc_mix: bfloat16 [65536, 4096], P(('grp', 'blk')), may hold values from 0.019897461 to 50
- word_topic: float32 [4096, 4096], P('blk'), may hold values from 0.01 to 8
- topic_total: float32 [4096], replicated, may hold values from 20000 to 400000
Outputs:
- doc_share: bfloat16 [65536, 4096], P(('grp', 'blk'))
- word_topic_new: float32 [4096, 4096], P('blk')
- topic_mean: float32 [4096], replicated
All inputs are finite; a program needn't handle non-finite values.
Results may differ from a plain program's by a relative error of at most 0.0004.
The roundings to bfloat16 on the way count: a program that leaves them out, or rounds other values in their place, can miss the bound.
Values may be sent and summed in bfloat16 or wider, within the bound.
A program may use at most 128 MiB of HBM per device.

v0:
```python
import jax
import jax.numpy as jnp
from jax import lax
from jax.sharding import PartitionSpec as P

VOCAB = 262144


alpha_prior = 0.1
beta_prior = 0.01


def passed_along(block, axis, distance):
    devices = range(lax.axis_size(axis))
    route = [((i - distance) % len(devices), i) for i in devices]
    return lax.ppermute(block, axis, route)


def tile_terms(operands):
    doc_rows, block_counts, visitor = operands
    normalizer = jnp.dot(doc_rows, visitor.T, preferred_element_type=jnp.float32)
    ratio = (block_counts / normalizer).astype(jnp.bfloat16)
    doc_part = jnp.dot(ratio, visitor, preferred_element_type=jnp.float32)
    word_part = jnp.dot(ratio.T, doc_rows, preferred_element_type=jnp.float32)
    return (doc_part, word_part)


def shard_terms(visitor, block_counts, doc_low):
    return tile_terms((doc_low, block_counts, visitor))


def local(counts, tile_live, doc_lengths, doc_mix, word_topic, topic_total):
    block_rows = word_topic.shape[0]
    visits = tile_live.shape[1]
    word_weight = (word_topic + beta_prior) / (topic_total + beta_prior * VOCAB)[None, :]
    word_low = word_weight.astype(jnp.bfloat16)
    mix_wide = doc_mix.astype(jnp.float32)
    doc_theta = mix_wide / jnp.sum(mix_wide, axis=1, keepdims=True)
    doc_weight = doc_lengths.astype(jnp.float32)[:, None] * doc_theta + alpha_prior
    doc_low = doc_weight.astype(jnp.bfloat16)
    live_full = jnp.repeat(jnp.repeat(tile_live, block_rows, axis=0), block_rows, axis=1)
    live_counts = counts.astype(jnp.float32) * live_full.astype(jnp.float32)
    window_len = jnp.sum(live_counts, axis=1)
    doc_proj = jnp.zeros((doc_low.shape[0], doc_low.shape[1]), jnp.float32)
    word_accum = jnp.zeros((block_rows, doc_low.shape[1]), jnp.float32)
    visitor = word_low
    for offset in range(visits):
        if offset > 0:
            visitor, word_accum = (
                passed_along(visitor.astype(jnp.float32), "blk", -1).astype(visitor.dtype),
                passed_along(word_accum, "blk", -1),
            )
        block_counts = live_counts[:, offset * block_rows : (offset + 1) * block_rows]
        doc_part, word_part = shard_terms(visitor, block_counts, doc_low)
        doc_proj = doc_proj + doc_part
        word_accum = word_accum + word_part
    word_accum = passed_along(word_accum, "blk", visits - 1)
    doc_new = doc_weight * doc_proj
    column_sum = jnp.sum(doc_new, axis=0)
    topic_count = doc_low.shape[1]
    doc_share = (
        topic_count * (doc_new + alpha_prior) / (window_len[:, None] + topic_count * alpha_prior)
    ).astype(jnp.bfloat16)
    word_sum = lax.psum(word_accum, "grp")
    topic_sum = lax.psum(column_sum, ("grp", "blk"))
    vocab_window = block_rows * lax.axis_size("blk")
    return (doc_share, word_weight * word_sum, topic_sum / vocab_window)


def solution(mesh):
    return jax.shard_map(
        local,
        mesh=mesh,
        in_specs=(
            P(("grp", "blk"), None),
            P(("grp", "blk"), None),
            P(("grp", "blk")),
            P(("grp", "blk"), None),
            P("blk", None),
            P(),
        ),
        out_specs=(P(("grp", "blk"), None), P("blk", None), P()),
        check_vma=False,
    )
```

profile of v0, /device:TPU:1, one launch (start us, length us, event | category | flops | bytes accessed | tf_op | source)
XLA Modules:
  0.0 514.8 jit_solution(7656554678656352072)
XLA Ops:
  7.2 0.8 convert_element_type.95
  8.1 2.0 convert_reduce_fusion
  10.0 0.7 broadcast_add_fusion
  10.7 1.0 fusion.8
  11.8 0.3 broadcast_in_dim.5
  12.1 0.3 fusion.38
  12.4 1.0 copy-done
  13.4 0.2 fusion.18
  13.7 0.7 fusion.9
  14.4 0.5 fusion.41
  14.9 3.3 collective-permute-start.7
  18.1 4.6 collective-permute-start
  22.7 29.8 %collective-permute-done = bf16[128,4096]{1,0:T(8,128)(2,1)S(1)} collective-permute-done((bf16[128,4096]{1,0:T(8,128)(2,1)S(1)}, bf16[128,4096]{1,0:T(8,128)(2,1)S(1)}, u32[]{:S(2)}, u32[]{:S(2)}) %collective-permute-start) | collective-permute-done | bytes 1048608 | tf_op jit(solution)/shard_map/ppermute | solution.py:16
  52.6 0.7 fusion.10
  53.3 0.5 convolution_add_fusion.2
  53.8 5.0 collective-permute-start.8
  58.9 4.0 collective-permute-start.1
  62.9 27.7 %collective-permute-done.1 = bf16[128,4096]{1,0:T(8,128)(2,1)S(1)} collective-permute-done((bf16[128,4096]{1,0:T(8,128)(2,1)S(1)}, bf16[128,4096]{1,0:T(8,128)(2,1)S(1)}, u32[]{:S(2)}, u32[]{:S(2)}) %collective-permute-start.1) | collective-permute-done | bytes 1048608 | tf_op jit(solution)/shard_map/ppermute | solution.py:16
  90.6 0.7 fusion.11
  91.3 0.5 fusion.42
  91.8 0.3 add.91
  92.1 7.1 %collective-permute-start.9 = (f32[128,4096]{1,0:T(8,128)S(1)}, f32[128,4096]{1,0:T(8,128)S(1)}, u32[]{:S(2)}, u32[]{:S(2)}) collective-permute-start(f32[128,4096]{1,0:T(8,128)S(1)} %add.91), channel_id=1, source_target_pairs={{1,0},{2,1},{3,2},{4,3},{5,4},{6,5},{7,6},{8,7},{9,8},{10,9},{11,1... | collective-permute-start | bytes 6291464 | tf_op jit(solution)/shard_map/ppermute | solution.py:16
  99.2 4.0 collective-permute-start.2
  103.2 25.6 %collective-permute-done.2 = bf16[128,4096]{1,0:T(8,128)(2,1)S(1)} collective-permute-done((bf16[128,4096]{1,0:T(8,128)(2,1)S(1)}, bf16[128,4096]{1,0:T(8,128)(2,1)S(1)}, u32[]{:S(2)}, u32[]{:S(2)}) %collective-permute-start.2) | collective-permute-done | bytes 1048608 | tf_op jit(solution)/shard_map/ppermute | solution.py:16
  128.9 0.7 fusion.12
  129.6 0.5 fusion.43
  130.1 0.3 add.92
  130.3 9.2 %collective-permute-start.10 = (f32[128,4096]{1,0:T(8,128)S(1)}, f32[128,4096]{1,0:T(8,128)S(1)}, u32[]{:S(2)}, u32[]{:S(2)}) collective-permute-start(f32[128,4096]{1,0:T(8,128)S(1)} %add.92), channel_id=1, source_target_pairs={{1,0},{2,1},{3,2},{4,3},{5,4},{6,5},{7,6},{8,7},{9,8},{10,9},{11,1... | collective-permute-start | bytes 6291464 | tf_op jit(solution)/shard_map/ppermute | solution.py:16
  139.6 4.0 collective-permute-start.3
  143.6 23.5 %collective-permute-done.3 = bf16[128,4096]{1,0:T(8,128)(2,1)S(1)} collective-permute-done((bf16[128,4096]{1,0:T(8,128)(2,1)S(1)}, bf16[128,4096]{1,0:T(8,128)(2,1)S(1)}, u32[]{:S(2)}, u32[]{:S(2)}) %collective-permute-start.3) | collective-permute-done | bytes 1048608 | tf_op jit(solution)/shard_map/ppermute | solution.py:16
  167.1 0.7 fusion.13
  167.8 0.5 fusion.44
  168.3 0.3 add.93
  168.6 11.4 %collective-permute-start.11 = (f32[128,4096]{1,0:T(8,128)S(1)}, f32[128,4096]{1,0:T(8,128)S(1)}, u32[]{:S(2)}, u32[]{:S(2)}) collective-permute-start(f32[128,4096]{1,0:T(8,128)S(1)} %add.93), channel_id=1, source_target_pairs={{1,0},{2,1},{3,2},{4,3},{5,4},{6,5},{7,6},{8,7},{9,8},{10,9},{11,1... | collective-permute-start | bytes 6291464 | tf_op jit(solution)/shard_map/ppermute | solution.py:16
  179.9 4.0 collective-permute-start.4
  183.9 21.4 %collective-permute-done.4 = bf16[128,4096]{1,0:T(8,128)(2,1)S(1)} collective-permute-done((bf16[128,4096]{1,0:T(8,128)(2,1)S(1)}, bf16[128,4096]{1,0:T(8,128)(2,1)S(1)}, u32[]{:S(2)}, u32[]{:S(2)}) %collective-permute-start.4) | collective-permute-done | bytes 1048608 | tf_op jit(solution)/shard_map/ppermute | solution.py:16
  205.3 0.7 fusion.14
  206.0 0.5 fusion.45
  206.5 0.3 add.94
  206.8 13.5 %collective-permute-start.12 = (f32[128,4096]{1,0:T(8,128)S(1)}, f32[128,4096]{1,0:T(8,128)S(1)}, u32[]{:S(2)}, u32[]{:S(2)}) collective-permute-start(f32[128,4096]{1,0:T(8,128)S(1)} %add.94), channel_id=1, source_target_pairs={{1,0},{2,1},{3,2},{4,3},{5,4},{6,5},{7,6},{8,7},{9,8},{10,9},{11,1... | collective-permute-start | bytes 6291464 | tf_op jit(solution)/shard_map/ppermute | solution.py:16
  220.3 4.0 collective-permute-start.5
  224.3 19.3 %collective-permute-done.5 = bf16[128,4096]{1,0:T(8,128)(2,1)S(1)} collective-permute-done((bf16[128,4096]{1,0:T(8,128)(2,1)S(1)}, bf16[128,4096]{1,0:T(8,128)(2,1)S(1)}, u32[]{:S(2)}, u32[]{:S(2)}) %collective-permute-start.5) | collective-permute-done | bytes 1048608 | tf_op jit(solution)/shard_map/ppermute | solution.py:16
  243.6 0.7 fusion.15
  244.3 0.5 fusion.46
  244.8 0.3 add.95
  245.0 15.6 %collective-permute-start.13 = (f32[128,4096]{1,0:T(8,128)S(1)}, f32[128,4096]{1,0:T(8,128)S(1)}, u32[]{:S(2)}, u32[]{:S(2)}) collective-permute-start(f32[128,4096]{1,0:T(8,128)S(1)} %add.95), channel_id=1, source_target_pairs={{1,0},{2,1},{3,2},{4,3},{5,4},{6,5},{7,6},{8,7},{9,8},{10,9},{11,1... | collective-permute-start | bytes 6291464 | tf_op jit(solution)/shard_map/ppermute | solution.py:16
  260.6 4.0 collective-permute-start.6
  264.6 0.7 fusion.40
  265.3 16.5 %collective-permute-done.6 = bf16[128,4096]{1,0:T(8,128)(2,1)S(1)} collective-permute-done((bf16[128,4096]{1,0:T(8,128)(2,1)S(1)}, bf16[128,4096]{1,0:T(8,128)(2,1)S(1)}, u32[]{:S(2)}, u32[]{:S(2)}) %collective-permute-start.6) | collective-permute-done | bytes 1048608 | tf_op jit(solution)/shard_map/ppermute | solution.py:16
  281.8 0.7 fusion.16
  282.5 0.5 fusion.47
  283.0 0.2 add.96
  283.2 7.8 %collective-permute-start.14 = (f32[128,4096]{1,0:T(8,128)S(1)}, f32[128,4096]{1,0:T(8,128)}, u32[]{:S(2)}, u32[]{:S(2)}) collective-permute-start(f32[128,4096]{1,0:T(8,128)S(1)} %add.96), channel_id=1, source_target_pairs={{25,0},{26,1},{27,2},{28,3},{29,4},{30,5},{31,6},{0,7},{1,8},{2,9}... | collective-permute-start | bytes 6291464 | tf_op jit(solution)/shard_map/ppermute | solution.py:16
  291.0 2.7 convolution_add_fusion.1
  293.7 2.6 fusion.52
  296.3 2.6 fusion.51
  298.9 2.7 fusion.50
  301.6 2.7 fusion.49
  304.3 2.6 fusion.48
  306.9 47.8 %collective-permute-done.14 = f32[128,4096]{1,0:T(8,128)} collective-permute-done((f32[128,4096]{1,0:T(8,128)S(1)}, f32[128,4096]{1,0:T(8,128)}, u32[]{:S(2)}, u32[]{:S(2)}) %collective-permute-start.14) | collective-permute-done | bytes 2097184 | tf_op jit(solution)/shard_map/ppermute | solution.py:16
  354.7 11.5 %fusion.39 = (f32[4096]{0:T(1024)S(1)}, bf16[256,4096]{1,0:T(8,128)(2,1)}) fusion(f32[256]{0:T(256)S(1)} %broadcast_add_fusion.1, f32[256,4096]{1,0:T(8,128)} %fusion.48, f32[256,4096]{1,0:T(8,128)} %fusion.49, f32[256,4096]{1,0:T(8,128)} %fusion.50, f32[256,4096]{1,0:T(8,128)} %fusion.51, f32[256,4096]{1,0:T(8,128)} %fusion.52, ...), kind=kOutput, calls=%fused_computation.64 | convolution fusion | flops 285208576 | bytes 30493696 | tf_op jit(solution)/shard_map/dot_general | solution.py:23
  366.2 137.9 %psum.15 = f32[4096]{0:T(1024)S(1)} all-reduce(f32[4096]{0:T(1024)S(1)} %get-tuple-element.5), channel_id=1, replica_groups=mesh['grp'=8,'blk'=32] {'grp','blk'}, use_global_device_ids=true, to_apply=%region_4.0 | all-reduce | flops 4096 | bytes 32768 | tf_op jit(solution)/shard_map/psum | solution.py:65
  504.2 0.6 broadcast_multiply_fusion
  504.8 3.2 fusion.17
  (20 shorter events, 0.1 us)
Async XLA Ops:
  7.2 3.6 copy-start.1
  7.2 2.8 copy-start.3
  7.2 497.6 %all-reduce.2.cloned.1.call-start = ((), (), s32[]{:S(2)}) async-start(), calls=%async_computation | async-start | bytes 4194304 | tf_op jit(solution)/shard_map/psum | solution.py:64
  10.7 1.4 copy-start.2
  11.8 1.6 copy-start
  14.9 38.4 %collective-permute-start.7 = (f32[128,4096]{1,0:T(8,128)S(1)}, f32[128,4096]{1,0:T(8,128)S(1)}, u32[]{:S(2)}, u32[]{:S(2)}) collective-permute-start(f32[128,4096]{1,0:T(8,128)S(1)} %fusion.41), channel_id=1, source_target_pairs={{1,0},{2,1},{3,2},{4,3},{5,4},{6,5},{7,6},{8,7},{9,8},{10,9},{11,1... | collective-permute-start | bytes 6291464 | tf_op jit(solution)/shard_map/ppermute | solution.py:16
  18.1 34.4 %collective-permute-start = (bf16[128,4096]{1,0:T(8,128)(2,1)S(1)}, bf16[128,4096]{1,0:T(8,128)(2,1)S(1)}, u32[]{:S(2)}, u32[]{:S(2)}) collective-permute-start(bf16[128,4096]{1,0:T(8,128)(2,1)S(1)} %fusion.18), channel_id=1, source_target_pairs={{1,0},{2,1},{3,2},{4,3},{5,4},{6,5},{7,6},{8,7},{9,8},{10,9},{11,1... | collective-permute-start | bytes 3145736 | tf_op jit(solution)/shard_map/ppermute | solution.py:16
  53.8 38.0 %collective-permute-start.8 = (f32[128,4096]{1,0:T(8,128)S(1)}, f32[128,4096]{1,0:T(8,128)S(1)}, u32[]{:S(2)}, u32[]{:S(2)}) collective-permute-start(f32[128,4096]{1,0:T(8,128)S(1)} %convolution_add_fusion.2), channel_id=1, source_target_pairs={{1,0},{2,1},{3,2},{4,3},{5,4},{6,5},{7,6},{8,7},{9,8},{10,9},{11,1... | collective-permute-start | bytes 6291464 | tf_op jit(solution)/shard_map/ppermute | solution.py:16
  58.9 31.7 %collective-permute-start.1 = (bf16[128,4096]{1,0:T(8,128)(2,1)S(1)}, bf16[128,4096]{1,0:T(8,128)(2,1)S(1)}, u32[]{:S(2)}, u32[]{:S(2)}) collective-permute-start(bf16[128,4096]{1,0:T(8,128)(2,1)S(1)} %collective-permute-done), channel_id=1, source_target_pairs={{1,0},{2,1},{3,2},{4,3},{5,4},{6,5},{7,6},{8,7},{9,8},{10,9},{11,1... | collective-permute-start | bytes 3145736 | tf_op jit(solution)/shard_map/ppermute | solution.py:16
  92.1 38.0 %collective-permute-start.9 = (f32[128,4096]{1,0:T(8,128)S(1)}, f32[128,4096]{1,0:T(8,128)S(1)}, u32[]{:S(2)}, u32[]{:S(2)}) collective-permute-start(f32[128,4096]{1,0:T(8,128)S(1)} %add.91), channel_id=1, source_target_pairs={{1,0},{2,1},{3,2},{4,3},{5,4},{6,5},{7,6},{8,7},{9,8},{10,9},{11,1... | collective-permute-start | bytes 6291464 | tf_op jit(solution)/shard_map/ppermute | solution.py:16
  99.2 29.6 %collective-permute-start.2 = (bf16[128,4096]{1,0:T(8,128)(2,1)S(1)}, bf16[128,4096]{1,0:T(8,128)(2,1)S(1)}, u32[]{:S(2)}, u32[]{:S(2)}) collective-permute-start(bf16[128,4096]{1,0:T(8,128)(2,1)S(1)} %collective-permute-done.1), channel_id=1, source_target_pairs={{1,0},{2,1},{3,2},{4,3},{5,4},{6,5},{7,6},{8,7},{9,8},{10,9},{11,1... | collective-permute-start | bytes 3145736 | tf_op jit(solution)/shard_map/ppermute | solution.py:16
  130.3 38.0 %collective-permute-start.10 = (f32[128,4096]{1,0:T(8,128)S(1)}, f32[128,4096]{1,0:T(8,128)S(1)}, u32[]{:S(2)}, u32[]{:S(2)}) collective-permute-start(f32[128,4096]{1,0:T(8,128)S(1)} %add.92), channel_id=1, source_target_pairs={{1,0},{2,1},{3,2},{4,3},{5,4},{6,5},{7,6},{8,7},{9,8},{10,9},{11,1... | collective-permute-start | bytes 6291464 | tf_op jit(solution)/shard_map/ppermute | solution.py:16
  139.6 27.5 %collective-permute-start.3 = (bf16[128,4096]{1,0:T(8,128)(2,1)S(1)}, bf16[128,4096]{1,0:T(8,128)(2,1)S(1)}, u32[]{:S(2)}, u32[]{:S(2)}) collective-permute-start(bf16[128,4096]{1,0:T(8,128)(2,1)S(1)} %collective-permute-done.2), channel_id=1, source_target_pairs={{1,0},{2,1},{3,2},{4,3},{5,4},{6,5},{7,6},{8,7},{9,8},{10,9},{11,1... | collective-permute-start | bytes 3145736 | tf_op jit(solution)/shard_map/ppermute | solution.py:16
  168.6 38.0 %collective-permute-start.11 = (f32[128,4096]{1,0:T(8,128)S(1)}, f32[128,4096]{1,0:T(8,128)S(1)}, u32[]{:S(2)}, u32[]{:S(2)}) collective-permute-start(f32[128,4096]{1,0:T(8,128)S(1)} %add.93), channel_id=1, source_target_pairs={{1,0},{2,1},{3,2},{4,3},{5,4},{6,5},{7,6},{8,7},{9,8},{10,9},{11,1... | collective-permute-start | bytes 6291464 | tf_op jit(solution)/shard_map/ppermute | solution.py:16
  179.9 25.4 %collective-permute-start.4 = (bf16[128,4096]{1,0:T(8,128)(2,1)S(1)}, bf16[128,4096]{1,0:T(8,128)(2,1)S(1)}, u32[]{:S(2)}, u32[]{:S(2)}) collective-permute-start(bf16[128,4096]{1,0:T(8,128)(2,1)S(1)} %collective-permute-done.3), channel_id=1, source_target_pairs={{1,0},{2,1},{3,2},{4,3},{5,4},{6,5},{7,6},{8,7},{9,8},{10,9},{11,1... | collective-permute-start | bytes 3145736 | tf_op jit(solution)/shard_map/ppermute | solution.py:16
  206.8 38.0 %collective-permute-start.12 = (f32[128,4096]{1,0:T(8,128)S(1)}, f32[128,4096]{1,0:T(8,128)S(1)}, u32[]{:S(2)}, u32[]{:S(2)}) collective-permute-start(f32[128,4096]{1,0:T(8,128)S(1)} %add.94), channel_id=1, source_target_pairs={{1,0},{2,1},{3,2},{4,3},{5,4},{6,5},{7,6},{8,7},{9,8},{10,9},{11,1... | collective-permute-start | bytes 6291464 | tf_op jit(solution)/shard_map/ppermute | solution.py:16
  220.3 23.3 %collective-permute-start.5 = (bf16[128,4096]{1,0:T(8,128)(2,1)S(1)}, bf16[128,4096]{1,0:T(8,128)(2,1)S(1)}, u32[]{:S(2)}, u32[]{:S(2)}) collective-permute-start(bf16[128,4096]{1,0:T(8,128)(2,1)S(1)} %collective-permute-done.4), channel_id=1, source_target_pairs={{1,0},{2,1},{3,2},{4,3},{5,4},{6,5},{7,6},{8,7},{9,8},{10,9},{11,1... | collective-permute-start | bytes 3145736 | tf_op jit(solution)/shard_map/ppermute | solution.py:16
  245.0 38.0 %collective-permute-start.13 = (f32[128,4096]{1,0:T(8,128)S(1)}, f32[128,4096]{1,0:T(8,128)S(1)}, u32[]{:S(2)}, u32[]{:S(2)}) collective-permute-start(f32[128,4096]{1,0:T(8,128)S(1)} %add.95), channel_id=1, source_target_pairs={{1,0},{2,1},{3,2},{4,3},{5,4},{6,5},{7,6},{8,7},{9,8},{10,9},{11,1... | collective-permute-start | bytes 6291464 | tf_op jit(solution)/shard_map/ppermute | solution.py:16
  260.6 21.2 %collective-permute-start.6 = (bf16[128,4096]{1,0:T(8,128)(2,1)S(1)}, bf16[128,4096]{1,0:T(8,128)(2,1)S(1)}, u32[]{:S(2)}, u32[]{:S(2)}) collective-permute-start(bf16[128,4096]{1,0:T(8,128)(2,1)S(1)} %collective-permute-done.5), channel_id=1, source_target_pairs={{1,0},{2,1},{3,2},{4,3},{5,4},{6,5},{7,6},{8,7},{9,8},{10,9},{11,1... | collective-permute-start | bytes 3145736 | tf_op jit(solution)/shard_map/ppermute | solution.py:16
  283.2 71.5 %collective-permute-start.14 = (f32[128,4096]{1,0:T(8,128)S(1)}, f32[128,4096]{1,0:T(8,128)}, u32[]{:S(2)}, u32[]{:S(2)}) collective-permute-start(f32[128,4096]{1,0:T(8,128)S(1)} %add.96), channel_id=1, source_target_pairs={{25,0},{26,1},{27,2},{28,3},{29,4},{30,5},{31,6},{0,7},{1,8},{2,9}... | collective-permute-start | bytes 6291464 | tf_op jit(solution)/shard_map/ppermute | solution.py:16
Sparse Core Ops, SparseCore 0:
  354.8 138.8 all-reduce.1
where the time goes:
time: 520 us; the launch traced here: 515 us
  waiting for transfers between devices  212 us (41%)
  blocking collectives  138 us (27%)
  starting transfers between devices  102 us (20%)
  matrix products  37.6 us (7%)
  between operations  14.3 us (3%)
  other arithmetic  10.4 us (2%)
    ppermute x15, waiting for transfers between devices, passed_along(): return lax.ppermute(block, axis, route)  212 us
    psum x1, blocking collectives, local(): topic_sum = lax.psum(column_sum, ('grp', 'blk'))  138 us
    ppermute x15, starting transfers between devices, passed_along(): return lax.ppermute(block, axis, route)  102 us
    dot_general x8, matrix products, tile_terms(): doc_part = jnp.dot(ratio, visitor, preferred_element_type=jnp.float32)  28.1 us
  transfers between devices with their start and end apart: 16, of which 8 were waited for; matrix products, arithmetic and copies ran while one was open for 7% of the time, Pallas kernels for 0%

commit v1 on v0

v1 whole, which is shorter than its diff:
```python
import jax
import jax.numpy as jnp
from jax import lax
from jax.experimental import pallas as pl
from jax.experimental.pallas import tpu as pltpu
from jax.sharding import PartitionSpec as P

VOCAB = 262144

alpha_prior = 0.1
beta_prior = 0.01

MESH = pl.DeviceIdType.MESH
F32 = jnp.float32
BF16 = jnp.bfloat16

DOCS = 256
WB = 128
K = 4096
SPAN = 8
SLOTS = 11
CH = 4
ROWS = WB // CH
KD = K // 8
KH = KD // 2


def place(x, h, z, a, c):
    return {"grp": x * 2 + h, "blk": (z * 2 + a) * 2 + c}


def kernel(
    counts,
    live,
    lengths,
    mix,
    topic,
    total,
    share,
    summed,
    mean,
    words,
    doc_low,
    scale,
    docs,
    ratio,
    ratio_t,
    part,
    near,
    far,
    acc,
    hop1,
    hop2,
    gathered,
    wlen,
    column,
    col_z,
    col_x,
    col_p,
    send_w,
    recv_w,
    send_d,
    recv_d,
    send_r,
    send_rf,
    recv_r,
    send_n,
    recv_n,
    send_f,
    recv_f,
    send_z,
    recv_z,
    send_g,
    recv_g,
    send_t,
    recv_tz,
    recv_tx,
    recv_tp,
):
    grp = lax.axis_index("grp")
    blk = lax.axis_index("blk")
    x = lax.div(grp, 2)
    h = lax.rem(grp, 2)
    z = lax.div(blk, 4)
    i = lax.rem(blk, 4)
    a = lax.div(i, 2)
    c = lax.rem(i, 2)
    i2 = 2 * (1 - a) + c

    def xo(dx):
        return lax.rem(x + dx, 4)

    def zo(dz):
        return lax.rem(z + dz + 8, 8)

    def ho(dh):
        return lax.rem(h + dh, 2)

    def ao(da):
        return lax.rem(a + da, 2)

    def co(dc):
        return lax.rem(c + dc, 2)

    def remote(src, dst, send, recv, x_=x, h_=h, z_=z, a_=a, c_=c):
        return pltpu.make_async_remote_copy(
            src_ref=src,
            dst_ref=dst,
            send_sem=send,
            recv_sem=recv,
            device_id=place(x_, h_, z_, a_, c_),
            device_id_type=MESH,
        )

    barrier = pltpu.get_barrier_semaphore()
    greeted = 0

    def greet(**where):
        at = dict(x=x, h=h, z=z, a=a, c=c)
        at.update(where)
        pl.semaphore_signal(barrier, inc=1, device_id=place(**at), device_id_type=MESH)

    for dz in range(1, 8):
        greet(z=zo(dz))
        greeted += 1
    for dh in range(2):
        for da in range(2):
            for dc in range(2):
                if dh + da + dc:
                    greet(h=ho(dh), a=ao(da), c=co(dc))
                    greeted += 1
    for dx in range(1, 4):
        for dh in range(2):
            for dc in range(2):
                greet(x=xo(dx), h=ho(dh), c=co(dc))
                greeted += 1

    def chunk(slot, r):
        return words.at[pl.ds(pl.multiple_of(slot * WB + r * ROWS, ROWS), ROWS), :]

    def to_z(j, r):
        slot = 4 * j + i
        return remote(chunk(slot, r), chunk(slot + 4, r), send_w.at[j, r, 0], recv_w.at[slot + 4, r], z_=zo(-1))

    def to_partner(j, r):
        slot = 4 * j + i
        return remote(chunk(slot, r), chunk(slot, r), send_w.at[j, r, 1], recv_w.at[slot, r], c_=1 - c)

    def to_y(j, r):
        slot = 4 * j + i
        side = jnp.where(r < CH // 2, h, 1 - h)
        return remote(
            chunk(slot, r), chunk(slot, r), send_w.at[j, r, 2], recv_w.at[slot, r], h_=side, a_=1 - a
        )

    def relay(j, r):
        slot = 4 * j + i2
        return remote(chunk(slot, r), chunk(slot, r), send_w.at[j, r, 3], recv_w.at[slot, r], c_=1 - c)

    def arrived(slot, r):
        return pltpu.make_async_copy(chunk(slot, r), chunk(slot, r), recv_w.at[slot, r])

    def column_copies(j, r, act):
        if j == 0:
            act(to_z(j, r))
        elif j == 1:
            @pl.when(i <= 2)
            def _():
                act(to_z(j, r))
        if j == 1:
            act(to_partner(j, r))
            act(to_y(j, r))
        else:
            @pl.when(c == (1 if j == 0 else 0))
            def _():
                act(to_partner(j, r))

            @pl.when(a == (1 if j == 0 else 0))
            def _():
                act(to_y(j, r))

    start = lambda copy: copy.start()
    drain = lambda copy: copy.wait_send()

    inverse = 1.0 / (total[...] + beta_prior * VOCAB)

    @pl.loop(0, CH)
    def _(r):
        rows = pl.ds(pl.multiple_of(r * ROWS, ROWS), ROWS)
        own = pl.ds(pl.multiple_of(i * WB + r * ROWS, ROWS), ROWS)
        words[own, :] = ((topic[rows, :] + beta_prior) * inverse).astype(BF16)

        @pl.when(r == 0)
        def _():
            pl.semaphore_wait(barrier, greeted)

        @pl.when(r > 0)
        def _():
            column_copies(0, r - 1, start)

    own_docs = lax.rem(blk, 2) + 2 * x

    @pl.loop(0, DOCS // 32)
    def _(n):
        rows = pl.ds(pl.multiple_of(n * 32, 32), 32)
        wide = mix[rows, :].astype(F32)
        factor = lengths[rows, :].astype(F32) / jnp.sum(wide, axis=1, keepdims=True)
        scale[rows, :] = factor
        doc_low[rows, :] = (wide * factor + alpha_prior).astype(BF16)

        @pl.when(n == 0)
        def _():
            column_copies(0, CH - 1, start)

    def doc_rows(q):
        return pl.ds(pl.multiple_of(q * DOCS, DOCS), DOCS)

    def topics(q):
        return pl.ds(pl.multiple_of(q * KD, KD), KD)

    def doc_copy(dx, dc):
        to = 2 * xo(dx) + co(dc)
        return remote(
            doc_low.at[:, topics(to)],
            docs.at[doc_rows(own_docs), :],
            send_d.at[dx, dc],
            recv_d.at[own_docs],
            x_=xo(dx),
            c_=co(dc),
        )

    others = [(dx, dc) for dx in range(4) for dc in range(2) if dx + dc]
    docs[doc_rows(own_docs), :] = doc_low[:, topics(own_docs)]
    for dx, dc in others:
        doc_copy(dx, dc).start()

    wlen[...] = jnp.zeros_like(wlen)
    for q in range(4):
        ratio_t[SPAN, :, 2 * q * DOCS : (2 * q + 1) * DOCS] = jnp.zeros((WB, DOCS), BF16)
        ratio_t[0, :, (2 * q + 1) * DOCS : (2 * q + 2) * DOCS] = jnp.zeros((WB, DOCS), BF16)

    def ratio_at(q, k):
        return ratio_t.at[k + lax.rem(q, 2), :, doc_rows(q)]

    def ratio_out(k, dx):
        return remote(
            ratio_at(own_docs, k), ratio_at(own_docs, k), send_r.at[k, dx], recv_r.at[own_docs, k], x_=xo(dx)
        )

    def ratio_over(k):
        return remote(
            ratio_at(own_docs, k), ratio_at(own_docs, k), send_r.at[k, 0], recv_r.at[own_docs, k], c_=1 - c
        )

    def ratio_relay(k, dx):
        q = 2 * xo(dx) + c
        return remote(ratio_at(q, k), ratio_at(q, k), send_rf.at[k, dx - 1], recv_r.at[q, k], c_=1 - c)

    def ratio_arrived(q, k):
        return pltpu.make_async_copy(ratio_at(q, k), ratio_at(q, k), recv_r.at[q, k])

    def meet(slot):
        k = slot - i
        block = words[pl.ds(pl.multiple_of(slot * WB, WB), WB), :]
        normalizer = lax.dot_general(
            doc_low[...], block, (((1,), (1,)), ((), ())), preferred_element_type=F32
        )
        at = pl.ds(pl.multiple_of(k * WB, WB), WB)
        half = DOCS // 2
        top = live[0, k].astype(F32)
        low = live[1, k].astype(F32)
        mask = jnp.where(lax.broadcasted_iota(jnp.int32, (DOCS, WB), 0) < half, top, low)
        kept = counts[:, at].astype(F32) * mask
        wide = kept / normalizer
        ratio_t[k + c, :, doc_rows(own_docs)] = wide.T.astype(BF16)
        ratio[:, at] = wide.astype(BF16)
        wlen[...] += kept
        for dx in range(1, 4):
            ratio_out(k, dx).start()
        ratio_over(k).start()

    def relay_ratio(k):
        for dx in range(1, 4):
            ratio_arrived(2 * xo(dx) + c, k).wait()
            ratio_relay(k, dx).start()

    meet(i)

    @pl.loop(1, SLOTS + 3)
    def _(t):
        @pl.when(t <= 4)
        def _():
            r = t - 1
            arrived(4 + i, r).wait()
            column_copies(1, r, start)

        @pl.when(jnp.logical_and(t == 2, a == 0))
        def _():
            for r in range(CH):
                arrived(i2, r).wait()
                relay(0, r).start()

        @pl.when(jnp.logical_and(t >= 2, t <= 5))
        def _():
            r = t - 2
            arrived(4 + i2, r).wait()
            relay(1, r).start()

        @pl.when(jnp.logical_and(jnp.logical_and(t >= 5, t <= 8), i <= 2))
        def _():
            r = t - 5
            arrived(8 + i, r).wait()
            column_copies(2, r, start)

        @pl.when(jnp.logical_and(jnp.logical_and(t >= 6, t <= 9), a == 1))
        def _():
            r = t - 6
            arrived(8 + i2, r).wait()
            relay(2, r).start()

        back = t - 3 - i

        @pl.when(jnp.logical_and(back >= 0, back < SPAN))
        def _():
            relay_ratio(back)

        slot = t - 1
        column_of = lax.rem(slot, 4)

        @pl.when(jnp.logical_and(slot > i, slot < i + SPAN))
        def _():
            @pl.when(jnp.logical_and(column_of != i, column_of != i2))
            def _():
                for r in range(CH):
                    arrived(slot, r).wait()

            meet(slot)

    for dx, dc in others:
        q = 2 * xo(dx) + co(dc)
        pltpu.make_async_copy(docs.at[doc_rows(q), :], docs.at[doc_rows(q), :], recv_d.at[q]).wait()

    @pl.loop(0, SPAN)
    def _(k):
        for dx in range(4):
            ratio_arrived(2 * xo(dx) + (1 - c), k).wait()

    def products(n):
        made = jnp.dot(ratio_t[n], docs[...], preferred_element_type=F32)
        part[n, 0] = made[:, :KH]
        part[n, 1] = made[:, KH:]

    def near_copy(m, side):
        n = m + 2 + 2 * lax.div(m, 2)
        return remote(
            part.at[n, side], near.at[h, m], send_n.at[m, side], recv_n.at[h, m], h_=side, a_=1 - a
        )

    def far_copy(m):
        n = m + 2 * lax.div(m, 2)
        return remote(part.at[n, 1 - h], far.at[m], send_f.at[m], recv_f.at[m], h_=1 - h)

    @pl.loop(0, 4)
    def _(m):
        products(m + 2 + 2 * lax.div(m, 2))
        for side in range(2):
            near_copy(m, side).start()

    @pl.loop(0, 5)
    def _(m):
        products(m + 2 * lax.div(m, 2))
        far_copy(m).start()

    length = jnp.sum(wlen[...], axis=1, keepdims=True)
    under = 1.0 / (length + K * alpha_prior)

    @pl.loop(0, K // 512)
    def _(n):
        at = pl.ds(pl.multiple_of(n * 512, 512), 512)
        proj = jnp.dot(
            ratio[...],
            words[pl.ds(pl.multiple_of(i * WB, WB), SPAN * WB), at],
            preferred_element_type=F32,
        )
        weight = mix[:, at].astype(F32) * scale[...] + alpha_prior
        new = weight * proj
        column[:, at] = jnp.sum(new, axis=0, keepdims=True)
        share[:, at] = (K * (new + alpha_prior) * under).astype(BF16)

    def topic_z(dz):
        return remote(column, col_z.at[z], send_t.at[0, dz], recv_tz.at[z], z_=zo(dz))

    col_z[z] = column[...]
    for dz in range(1, 8):
        topic_z(dz).start()

    def wait_far(m):
        pltpu.make_async_copy(far.at[m], far.at[m], recv_f.at[m]).wait()

    def wait_near(m):
        for side in range(2):
            pltpu.make_async_copy(near.at[side, m], near.at[side, m], recv_n.at[side, m]).wait()

    def hop_copy(stage, q):
        source, target = ((4, hop1), (2, hop2))[stage]
        return remote(acc.at[source + q], target.at[q], send_z.at[stage, q], recv_z.at[stage, q], z_=zo(1))

    def hop_arrived(stage, q):
        target = (hop1, hop2)[stage]
        return pltpu.make_async_copy(target.at[q], target.at[q], recv_z.at[stage, q])

    wait_far(4)
    acc[4] = part[8, h] + far[4]

    @pl.when(a == 0)
    def _():
        for q in (4, 5):
            wait_near(q - 2)
        acc[4] += near[0, 2] + near[1, 2]
        acc[5] = near[0, 3] + near[1, 3]
        hop_copy(0, 1).start()

    hop_copy(0, 0).start()

    for q in (2, 3):
        wait_far(q)
        acc[q] = part[(4, 5)[q - 2], h] + far[q]
        m = q - 2 + 2 * a
        wait_near(m)
        acc[q] += near[0, m] + near[1, m]
    for q in (0, 1):
        wait_far(q)
        acc[q] = part[q, h] + far[q]

        @pl.when(a == 1)
        def _():
            wait_near(q)
            acc[q] += near[0, q] + near[1, q]

    hop_arrived(0, 0).wait()
    acc[2] += hop1[0]

    @pl.when(a == 0)
    def _():
        hop_arrived(0, 1).wait()
        acc[3] += hop1[1]

    for q in range(2):
        hop_copy(1, q).start()

    for dz in range(1, 8):
        q = zo(dz)
        pltpu.make_async_copy(col_z.at[q], col_z.at[q], recv_tz.at[q]).wait()
    column_z = col_z[0]
    for q in range(1, 8):
        column_z += col_z[q]
    col_x[x] = column_z

    def topic_x(dx):
        return remote(col_x.at[x], col_x.at[x], send_t.at[1, dx], recv_tx.at[x], x_=xo(dx))

    for dx in range(1, 4):
        topic_x(dx).start()

    for q in range(2):
        hop_arrived(1, q).wait()
        acc[q] += hop2[q]

    def piece(q, h_):
        return pl.ds(pl.multiple_of(q * KD + h_ * KH, KH), KH)

    def gather_copy(dx, dh, dc):
        return remote(
            acc.at[co(dc)],
            gathered.at[:, piece(own_docs, h)],
            send_g.at[dx, dh, dc],
            recv_g.at[own_docs, h],
            x_=xo(dx),
            h_=ho(dh),
            c_=co(dc),
        )

    fan = [(dx, dh, dc) for dx in (2, 1, 3, 0) for dh in range(2) for dc in range(2) if dx + dh + dc]
    for where in fan:
        gather_copy(*where).start()
    gathered[:, piece(own_docs, h)] = acc[c]

    for dx in range(1, 4):
        q = xo(dx)
        pltpu.make_async_copy(col_x.at[q], col_x.at[q], recv_tx.at[q]).wait()
    column_x = col_x[0]
    for q in range(1, 4):
        column_x += col_x[q]
    me = h * 4 + i
    col_p[me] = column_x

    def topic_p(dh, da, dc):
        return remote(
            col_p.at[me],
            col_p.at[me],
            send_t.at[2, 4 * dh + 2 * da + dc],
            recv_tp.at[me],
            h_=ho(dh),
            a_=ao(da),
            c_=co(dc),
        )

    plane = [(dh, da, dc) for dh in range(2) for da in range(2) for dc in range(2) if dh + da + dc]
    for where in plane:
        topic_p(*where).start()

    for dh, da, dc in plane:
        q = 4 * ho(dh) + 2 * ao(da) + co(dc)
        pltpu.make_async_copy(col_p.at[q], col_p.at[q], recv_tp.at[q]).wait()
    column_p = col_p[0]
    for q in range(1, 8):
        column_p += col_p[q]
    mean[...] = column_p * (1.0 / (WB * 32))

    for dx, dh, dc in fan:
        q = 2 * xo(dx) + co(dc)
        at = gathered.at[:, piece(q, ho(dh))]
        pltpu.make_async_copy(at, at, recv_g.at[q, ho(dh)]).wait()
    summed[...] = gathered[...]

    @pl.loop(0, CH)
    def _(r):
        column_copies(0, r, drain)
        column_copies(1, r, drain)

        @pl.when(i <= 2)
        def _():
            column_copies(2, r, drain)

        @pl.when(a == 0)
        def _():
            drain(relay(0, r))

        drain(relay(1, r))

        @pl.when(a == 1)
        def _():
            drain(relay(2, r))

    for dx, dc in others:
        drain(doc_copy(dx, dc))

    @pl.loop(0, SPAN)
    def _(k):
        for dx in range(1, 4):
            drain(ratio_out(k, dx))
            drain(ratio_relay(k, dx))
        drain(ratio_over(k))

    @pl.loop(0, 4)
    def _(m):
        for side in range(2):
            drain(near_copy(m, side))

    @pl.loop(0, 5)
    def _(m):
        drain(far_copy(m))

    drain(hop_copy(0, 0))

    @pl.when(a == 0)
    def _():
        drain(hop_copy(0, 1))

    for q in range(2):
        drain(hop_copy(1, q))
    for where in fan:
        drain(gather_copy(*where))
    for dz in range(1, 8):
        drain(topic_z(dz))
    for dx in range(1, 4):
        drain(topic_x(dx))
    for where in plane:
        drain(topic_p(*where))


def exchange(counts, tile_live, lengths, doc_mix, word_topic, topic_total):
    vmem = pl.BlockSpec(memory_space=pltpu.VMEM)
    smem = pl.BlockSpec(memory_space=pltpu.SMEM)
    dma = pltpu.SemaphoreType.DMA
    return pl.pallas_call(
        kernel,
        name="window",
        out_shape=(
            jax.ShapeDtypeStruct((DOCS, K), BF16),
            jax.ShapeDtypeStruct((WB, K), F32),
            jax.ShapeDtypeStruct((1, K), F32),
        ),
        in_specs=[vmem, smem, vmem, vmem, vmem, vmem],
        out_specs=(vmem, vmem, vmem),
        scratch_shapes=[
            pltpu.VMEM((SLOTS * WB, K), BF16),
            pltpu.VMEM((DOCS, K), BF16),
            pltpu.VMEM((DOCS, 1), F32),
            pltpu.VMEM((8 * DOCS, KD), BF16),
            pltpu.VMEM((DOCS, SPAN * WB), BF16),
            pltpu.VMEM((SPAN + 1, WB, 8 * DOCS), BF16),
            pltpu.VMEM((SPAN + 1, 2, WB, KH), F32),
            pltpu.VMEM((2, 4, WB, KH), F32),
            pltpu.VMEM((5, WB, KH), F32),
            pltpu.VMEM((6, WB, KH), F32),
            pltpu.VMEM((2, WB, KH), F32),
            pltpu.VMEM((2, WB, KH), F32),
            pltpu.VMEM((WB, K), F32),
            pltpu.VMEM((DOCS, WB), F32),
            pltpu.VMEM((1, K), F32),
            pltpu.VMEM((8, 1, K), F32),
            pltpu.VMEM((4, 1, K), F32),
            pltpu.VMEM((8, 1, K), F32),
            dma((3, CH, 4)),
            dma((SLOTS, CH)),
            dma((4, 2)),
            dma((8,)),
            dma((SPAN, 4)),
            dma((SPAN, 3)),
            dma((8, SPAN)),
            dma((4, 2)),
            dma((2, 4)),
            dma((5,)),
            dma((5,)),
            dma((2, 2)),
            dma((2, 2)),
            dma((4, 2, 2)),
            dma((8, 2)),
            dma((3, 8)),
            dma((8,)),
            dma((4,)),
            dma((8,)),
        ],
        compiler_params=pltpu.CompilerParams(
            collective_id=0, has_side_effects=True, vmem_limit_bytes=60 * 1024 * 1024
        ),
    )(counts, tile_live, lengths, doc_mix, word_topic, topic_total)


def local(counts, tile_live, doc_lengths, doc_mix, word_topic, topic_total):
    doc_share, word_sum, topic_mean = exchange(
        counts, tile_live, doc_lengths[:, None], doc_mix, word_topic, topic_total[None, :]
    )
    word_weight = (word_topic + beta_prior) / (topic_total + beta_prior * VOCAB)[None, :]
    return (doc_share, word_weight * word_sum, topic_mean[0])


def solution(mesh):
    return jax.shard_map(
        local,
        mesh=mesh,
        in_specs=(
            P(("grp", "blk"), None),
            P(("grp", "blk"), None),
            P(("grp", "blk")),
            P(("grp", "blk"), None),
            P("blk", None),
            P(),
        ),
        out_specs=(P(("grp", "blk"), None), P("blk", None), P()),
        check_vma=False,
    )
```

time: 520 us -> 163 us (0.31)
  waiting for transfers between devices: 212 us -> 0 us
  Pallas kernels: 0 us -> 155 us
  blocking collectives: 138 us -> 0 us
  starting transfers between devices: 102 us -> 0 us
  matrix products: 37.6 us -> 0 us
  between operations: 14.3 us -> 0.66 us
  other arithmetic: 10.4 us -> 4.13 us
    ppermute x15 -> x0, waiting for transfers between devices: 212 us -> none  [passed_along(): return lax.ppermute(block, axis, route)]
    pallas_call x0 -> x1, Pallas kernels: none -> 155 us  [exchange(): pl.pallas_call(kernel, name='window', out_shape=(jax.ShapeDtypeStruct((DO...]
    psum x1 -> x0, blocking collectives: 138 us -> none  [local(): topic_sum = lax.psum(column_sum, ('grp', 'blk'))]
    ppermute x15 -> x0, starting transfers between devices: 102 us -> none  [passed_along(): return lax.ppermute(block, axis, route)]
    dot_general x24 -> x0, matrix products: 37.6 us -> none  [the longest x8 28.1 us: tile_terms(): doc_part = jnp.dot(ratio, visitor, preferred_element_type=jnp.float32)]
  transfers between devices with their start and end apart: 16 -> 0, of which waited for: 8 -> 0; matrix products, arithmetic and copies ran while one was open for 7% -> 0% of each run, Pallas kernels for 0% -> 0%
where the time goes in v1:
time: 163 us
  Pallas kernels  155 us (95%)
  other arithmetic  4.13 us (3%)
  local copies, waits for them, and re-layouts  3.41 us (2%)
    pallas_call x1, Pallas kernels, exchange(): pl.pallas_call(kernel, name='window', out_shape=(jax.ShapeDtypeStruct((DO...  155 us
    mul x1, other arithmetic, local(): return (doc_share, word_weight * word_sum, topic_mean[0])  3.4 us

profile of v1, /device:TPU:1, one launch (start us, length us, event | category | flops | bytes accessed | tf_op | source)
XLA Modules:
  0.0 163.0 jit_solution(18418207091210553868)
XLA Ops:
  0.6 0.7 broadcast_add_fusion
  1.4 1.5 copy.9.lengths
  2.8 0.0 copy-start
  2.8 154.8 %window.1 = (bf16[256,4096]{1,0:T(8,128)(2,1)}, f32[128,4096]{1,0:T(8,128)}, f32[1,4096]{1,0:T(1,128)}) custom-call(s32[256,1024]{1,0:T(8,128)} %counts.1, s32[2,8]{1,0:T(2,128)} %live.1, s32[256,1]{1,0:T(8,128)} %copy.9.lengths, bf16[256,4096]{1,0:T(8,128)(2,1)} %mix.1, f32[128,4096]{1,0:T(8,128)} %topic.1, f32[1,4096]{1,0:T(1,128)} %bitcast.3), custom_call_target="tpu_custom_call" | custom-call | tf_op jit(solution)/shard_map/window/pallas_call | solution.py:586
  157.6 0.0 copy-done
  157.7 0.0 copy-start.1
  157.7 3.4 %divide_multiply_fusion = f32[128,4096]{1,0:T(8,128)} fusion(f32[128,4096]{1,0:T(8,128)} %get-tuple-element.7, f32[128,4096]{1,0:T(8,128)S(1)} %copy-done, f32[4096]{0:T(1024)S(1)} %broadcast_add_fusion), kind=kLoop, calls=%fused_computation | loop fusion | flops 1572864 | bytes 6307840 | tf_op jit(solution)/shard_map/mul | solution.py:646
  161.1 0.0 copy-done.1
  161.1 0.0 copy-start.2
  161.1 1.3 copy.12
  162.4 0.0 copy-done.2
  162.4 0.6 copy.13
Async XLA Ops:
  2.8 154.8 %copy-start = (f32[128,4096]{1,0:T(8,128)S(1)}, f32[128,4096]{1,0:T(8,128)}, u32[]{:S(2)}) copy-start(f32[128,4096]{1,0:T(8,128)} %topic.1) | copy-start | bytes 6291460
  157.7 3.4 %copy-start.1 = (bf16[256,4096]{1,0:T(8,128)(2,1)S(1)}, bf16[256,4096]{1,0:T(8,128)(2,1)}, u32[]{:S(2)}) copy-start(bf16[256,4096]{1,0:T(8,128)(2,1)} %get-tuple-element.12) | copy-start | bytes 6291460
  161.1 1.3 copy-start.2

commit v2 on v1

--- a/solution.py
+++ b/solution.py
@@ -23,6 +23,7 @@
 ROWS = WB // CH
 KD = K // 8
 KH = KD // 2
+PARTS = 2
 
 
 def place(x, h, z, a, c):
@@ -30,15 +31,21 @@
 
 
 def kernel(
-    counts,
+    counts_in,
     live,
     lengths,
+    mix_in,
+    topic_in,
+    total,
+    share_out,
+    topic_out,
+    mean,
+    counts,
     mix,
     topic,
-    total,
     share,
-    summed,
-    mean,
+    inverse,
+    span,
     words,
     doc_low,
     scale,
@@ -76,6 +83,8 @@
     recv_tz,
     recv_tx,
     recv_tp,
+    load,
+    store,
 ):
     grp = lax.axis_index("grp")
     blk = lax.axis_index("blk")
@@ -111,6 +120,17 @@
             device_id=place(x_, h_, z_, a_, c_),
             device_id_type=MESH,
         )
+
+    def topic_load(r):
+        rows = pl.ds(pl.multiple_of(r * ROWS, ROWS), ROWS)
+        return pltpu.make_async_copy(topic_in.at[rows, :], topic.at[rows, :], load.at[r])
+
+    mix_load = pltpu.make_async_copy(mix_in, mix, load.at[CH])
+    counts_load = pltpu.make_async_copy(counts_in, counts, load.at[CH + 1])
+    for r in range(CH):
+        topic_load(r).start()
+    mix_load.start()
+    counts_load.start()
 
     barrier = pltpu.get_barrier_semaphore()
     greeted = 0
@@ -182,13 +202,17 @@
     start = lambda copy: copy.start()
     drain = lambda copy: copy.wait_send()
 
-    inverse = 1.0 / (total[...] + beta_prior * VOCAB)
+    inverse[...] = 1.0 / (total[...] + beta_prior * VOCAB)
+    span[...] = jnp.broadcast_to(lengths[...].astype(F32), (8, DOCS)).T[:, :1]
 
     @pl.loop(0, CH)
     def _(r):
         rows = pl.ds(pl.multiple_of(r * ROWS, ROWS), ROWS)
         own = pl.ds(pl.multiple_of(i * WB + r * ROWS, ROWS), ROWS)
-        words[own, :] = ((topic[rows, :] + beta_prior) * inverse).astype(BF16)
+        topic_load(r).wait()
+        weight = (topic[rows, :] + beta_prior) * inverse[...]
+        topic[rows, :] = weight
+        words[own, :] = weight.astype(BF16)
 
         @pl.when(r == 0)
         def _():
@@ -198,13 +222,14 @@
         def _():
             column_copies(0, r - 1, start)
 
-    own_docs = lax.rem(blk, 2) + 2 * x
+    own_docs = 2 * x + c
+    mix_load.wait()
 
     @pl.loop(0, DOCS // 32)
     def _(n):
         rows = pl.ds(pl.multiple_of(n * 32, 32), 32)
         wide = mix[rows, :].astype(F32)
-        factor = lengths[rows, :].astype(F32) / jnp.sum(wide, axis=1, keepdims=True)
+        factor = span[rows, :] / jnp.sum(wide, axis=1, keepdims=True)
         scale[rows, :] = factor
         doc_low[rows, :] = (wide * factor + alpha_prior).astype(BF16)
 
@@ -284,9 +309,48 @@
             ratio_arrived(2 * xo(dx) + c, k).wait()
             ratio_relay(k, dx).start()
 
+    def near_copy(m, side):
+        n = m + 2 + 2 * lax.div(m, 2)
+        return remote(
+            part.at[n, side], near.at[h, m], send_n.at[m, side], recv_n.at[h, m], h_=side, a_=1 - a
+        )
+
+    def far_copy(m):
+        n = m + 2 * lax.div(m, 2)
+        return remote(part.at[n, 1 - h], far.at[m], send_f.at[m], recv_f.at[m], h_=1 - h)
+
+    def products(n):
+        @pl.when(n == 0)
+        def _():
+            for dx, dc in others:
+                q = 2 * xo(dx) + co(dc)
+                pltpu.make_async_copy(docs.at[doc_rows(q), :], docs.at[doc_rows(q), :], recv_d.at[q]).wait()
+
+        k = n - (1 - c)
+
+        @pl.when(jnp.logical_and(k >= 0, k < SPAN))
+        def _():
+            for dx in range(4):
+                ratio_arrived(2 * xo(dx) + (1 - c), k).wait()
+
+        made = jnp.dot(ratio_t[n], docs[...], preferred_element_type=F32)
+        part[n, 0] = made[:, :KH]
+        part[n, 1] = made[:, KH:]
+        m = n - 2 * lax.div(n, 4)
+
+        @pl.when(lax.rem(lax.div(n, 2), 2) == 1)
+        def _():
+            for side in range(2):
+                near_copy(m - 2, side).start()
+
+        @pl.when(lax.rem(lax.div(n, 2), 2) == 0)
+        def _():
+            far_copy(m).start()
+
+    counts_load.wait()
     meet(i)
 
-    @pl.loop(1, SLOTS + 3)
+    @pl.loop(1, SLOTS + 4)
     def _(t):
         @pl.when(t <= 4)
         def _():
@@ -323,6 +387,12 @@
         @pl.when(jnp.logical_and(back >= 0, back < SPAN))
         def _():
             relay_ratio(back)
+
+        ready = t - 4 - 2 * a
+
+        @pl.when(jnp.logical_and(ready >= 0, ready <= SPAN))
+        def _():
+            products(ready)
 
         slot = t - 1
         column_of = lax.rem(slot, 4)
@@ -335,41 +405,6 @@
                     arrived(slot, r).wait()
 
             meet(slot)
-
-    for dx, dc in others:
-        q = 2 * xo(dx) + co(dc)
-        pltpu.make_async_copy(docs.at[doc_rows(q), :], docs.at[doc_rows(q), :], recv_d.at[q]).wait()
-
-    @pl.loop(0, SPAN)
-    def _(k):
-        for dx in range(4):
-            ratio_arrived(2 * xo(dx) + (1 - c), k).wait()
-
-    def products(n):
-        made = jnp.dot(ratio_t[n], docs[...], preferred_element_type=F32)
-        part[n, 0] = made[:, :KH]
-        part[n, 1] = made[:, KH:]
-
-    def near_copy(m, side):
-        n = m + 2 + 2 * lax.div(m, 2)
-        return remote(
-            part.at[n, side], near.at[h, m], send_n.at[m, side], recv_n.at[h, m], h_=side, a_=1 - a
-        )
-
-    def far_copy(m):
-        n = m + 2 * lax.div(m, 2)
-        return remote(part.at[n, 1 - h], far.at[m], send_f.at[m], recv_f.at[m], h_=1 - h)
-
-    @pl.loop(0, 4)
-    def _(m):
-        products(m + 2 + 2 * lax.div(m, 2))
-        for side in range(2):
-            near_copy(m, side).start()
-
-    @pl.loop(0, 5)
-    def _(m):
-        products(m + 2 * lax.div(m, 2))
-        far_copy(m).start()
 
     length = jnp.sum(wlen[...], axis=1, keepdims=True)
     under = 1.0 / (length + K * alpha_prior)
@@ -387,6 +422,9 @@
         column[:, at] = jnp.sum(new, axis=0, keepdims=True)
         share[:, at] = (K * (new + alpha_prior) * under).astype(BF16)
 
+    share_store = pltpu.make_async_copy(share, share_out, store.at[2])
+    share_store.start()
+
     def topic_z(dz):
         return remote(column, col_z.at[z], send_t.at[0, dz], recv_tz.at[z], z_=zo(dz))
 
@@ -401,13 +439,22 @@
         for side in range(2):
             pltpu.make_async_copy(near.at[side, m], near.at[side, m], recv_n.at[side, m]).wait()
 
-    def hop_copy(stage, q):
+    def part_rows(p):
+        return slice(p * WB // PARTS, (p + 1) * WB // PARTS)
+
+    def hop_copy(stage, q, p):
         source, target = ((4, hop1), (2, hop2))[stage]
-        return remote(acc.at[source + q], target.at[q], send_z.at[stage, q], recv_z.at[stage, q], z_=zo(1))
-
-    def hop_arrived(stage, q):
-        target = (hop1, hop2)[stage]
-        return pltpu.make_async_copy(target.at[q], target.at[q], recv_z.at[stage, q])
+        return remote(
+            acc.at[source + q, part_rows(p), :],
+            target.at[q, part_rows(p), :],
+            send_z.at[stage, q, p],
+            recv_z.at[stage, q, p],
+            z_=zo(1),
+        )
+
+    def hop_arrived(stage, q, p):
+        at = (hop1, hop2)[stage].at[q, part_rows(p), :]
+        return pltpu.make_async_copy(at, at, recv_z.at[stage, q, p])
 
     wait_far(4)
     acc[4] = part[8, h] + far[4]
@@ -418,9 +465,11 @@
             wait_near(q - 2)
         acc[4] += near[0, 2] + near[1, 2]
         acc[5] = near[0, 3] + near[1, 3]
-        hop_copy(0, 1).start()
-
-    hop_copy(0, 0).start()
+        for p in range(PARTS):
+            hop_copy(0, 1, p).start()
+
+    for p in range(PARTS):
+        hop_copy(0, 0, p).start()
 
     for q in (2, 3):
         wait_far(q)
@@ -437,16 +486,18 @@
             wait_near(q)
             acc[q] += near[0, q] + near[1, q]
 
-    hop_arrived(0, 0).wait()
-    acc[2] += hop1[0]
-
-    @pl.when(a == 0)
-    def _():
-        hop_arrived(0, 1).wait()
-        acc[3] += hop1[1]
-
-    for q in range(2):
-        hop_copy(1, q).start()
+    for p in range(PARTS):
+        rows = part_rows(p)
+        hop_arrived(0, 0, p).wait()
+        acc[2, rows] += hop1[0, rows]
+
+        @pl.when(a == 0)
+        def _():
+            hop_arrived(0, 1, p).wait()
+            acc[3, rows] += hop1[1, rows]
+
+        for q in range(2):
+            hop_copy(1, q, p).start()
 
     for dz in range(1, 8):
         q = zo(dz)
@@ -462,28 +513,29 @@
     for dx in range(1, 4):
         topic_x(dx).start()
 
-    for q in range(2):
-        hop_arrived(1, q).wait()
-        acc[q] += hop2[q]
-
     def piece(q, h_):
         return pl.ds(pl.multiple_of(q * KD + h_ * KH, KH), KH)
 
-    def gather_copy(dx, dh, dc):
+    def gather_copy(p, dx, dh, dc):
         return remote(
-            acc.at[co(dc)],
-            gathered.at[:, piece(own_docs, h)],
-            send_g.at[dx, dh, dc],
-            recv_g.at[own_docs, h],
+            acc.at[co(dc), part_rows(p), :],
+            gathered.at[part_rows(p), piece(own_docs, h)],
+            send_g.at[p, dx, dh, dc],
+            recv_g.at[p, own_docs, h],
             x_=xo(dx),
             h_=ho(dh),
             c_=co(dc),
         )
 
     fan = [(dx, dh, dc) for dx in (2, 1, 3, 0) for dh in range(2) for dc in range(2) if dx + dh + dc]
-    for where in fan:
-        gather_copy(*where).start()
-    gathered[:, piece(own_docs, h)] = acc[c]
+    for p in range(PARTS):
+        rows = part_rows(p)
+        for q in range(2):
+            hop_arrived(1, q, p).wait()
+            acc[q, rows] += hop2[q, rows]
+        gathered[rows, piece(own_docs, h)] = acc[c, rows]
+        for where in fan:
+            gather_copy(p, *where).start()
 
     for dx in range(1, 4):
         q = xo(dx)
@@ -517,11 +569,17 @@
         column_p += col_p[q]
     mean[...] = column_p * (1.0 / (WB * 32))
 
-    for dx, dh, dc in fan:
-        q = 2 * xo(dx) + co(dc)
-        at = gathered.at[:, piece(q, ho(dh))]
-        pltpu.make_async_copy(at, at, recv_g.at[q, ho(dh)]).wait()
-    summed[...] = gathered[...]
+    def topic_store(p):
+        return pltpu.make_async_copy(gathered.at[part_rows(p), :], topic_out.at[part_rows(p), :], store.at[p])
+
+    for p in range(PARTS):
+        rows = part_rows(p)
+        for dx, dh, dc in fan:
+            q = 2 * xo(dx) + co(dc)
+            at = gathered.at[rows, piece(q, ho(dh))]
+            pltpu.make_async_copy(at, at, recv_g.at[p, q, ho(dh)]).wait()
+        gathered[rows, :] = gathered[rows, :] * topic[rows, :]
+        topic_store(p).start()
 
     @pl.loop(0, CH)
     def _(r):
@@ -561,26 +619,31 @@
     def _(m):
         drain(far_copy(m))
 
-    drain(hop_copy(0, 0))
-
-    @pl.when(a == 0)
-    def _():
-        drain(hop_copy(0, 1))
-
-    for q in range(2):
-        drain(hop_copy(1, q))
-    for where in fan:
-        drain(gather_copy(*where))
+    for p in range(PARTS):
+        drain(hop_copy(0, 0, p))
+
+        @pl.when(a == 0)
+        def _():
+            drain(hop_copy(0, 1, p))
+
+        for q in range(2):
+            drain(hop_copy(1, q, p))
+        for where in fan:
+            drain(gather_copy(p, *where))
     for dz in range(1, 8):
         drain(topic_z(dz))
     for dx in range(1, 4):
         drain(topic_x(dx))
     for where in plane:
         drain(topic_p(*where))
+    share_store.wait()
+    for p in range(PARTS):
+        topic_store(p).wait()
 
 
 def exchange(counts, tile_live, lengths, doc_mix, word_topic, topic_total):
     vmem = pl.BlockSpec(memory_space=pltpu.VMEM)
+    hbm = pl.BlockSpec(memory_space=pltpu.HBM)
     smem = pl.BlockSpec(memory_space=pltpu.SMEM)
     dma = pltpu.SemaphoreType.DMA
     return pl.pallas_call(
@@ -591,9 +654,15 @@
             jax.ShapeDtypeStruct((WB, K), F32),
             jax.ShapeDtypeStruct((1, K), F32),
         ),
-        in_specs=[vmem, smem, vmem, vmem, vmem, vmem],
-        out_specs=(vmem, vmem, vmem),
+        in_specs=[hbm, smem, vmem, hbm, hbm, vmem],
+        out_specs=(hbm, hbm, vmem),
         scratch_shapes=[
+            pltpu.VMEM((DOCS, SPAN * WB), jnp.int32),
+            pltpu.VMEM((DOCS, K), BF16),
+            pltpu.VMEM((WB, K), F32),
+            pltpu.VMEM((DOCS, K), BF16),
+            pltpu.VMEM((1, K), F32),
+            pltpu.VMEM((DOCS, 1), F32),
             pltpu.VMEM((SLOTS * WB, K), BF16),
             pltpu.VMEM((DOCS, K), BF16),
             pltpu.VMEM((DOCS, 1), F32),
@@ -623,14 +692,16 @@
             dma((2, 4)),
             dma((5,)),
             dma((5,)),
-            dma((2, 2)),
-            dma((2, 2)),
-            dma((4, 2, 2)),
-            dma((8, 2)),
+            dma((2, 2, PARTS)),
+            dma((2, 2, PARTS)),
+            dma((PARTS, 4, 2, 2)),
+            dma((PARTS, 8, 2)),
             dma((3, 8)),
             dma((8,)),
             dma((4,)),
             dma((8,)),
+            dma((CH + 2,)),
+            dma((PARTS + 1,)),
         ],
         compiler_params=pltpu.CompilerParams(
             collective_id=0, has_side_effects=True, vmem_limit_bytes=60 * 1024 * 1024
@@ -639,11 +710,10 @@
 
 
 def local(counts, tile_live, doc_lengths, doc_mix, word_topic, topic_total):
-    doc_share, word_sum, topic_mean = exchange(
-        counts, tile_live, doc_lengths[:, None], doc_mix, word_topic, topic_total[None, :]
+    doc_share, topic_new, topic_mean = exchange(
+        counts, tile_live, doc_lengths[None, :], doc_mix, word_topic, topic_total[None, :]
     )
-    word_weight = (word_topic + beta_prior) / (topic_total + beta_prior * VOCAB)[None, :]
-    return (doc_share, word_weight * word_sum, topic_mean[0])
+    return (doc_share, topic_new, topic_mean[0])
 
 
 def solution(mesh):

time: 163 us -> 146 us (0.90)
  Pallas kernels: 155 us -> 140 us
  other arithmetic: 4.13 us -> 0 us
  local copies, waits for them, and re-layouts: 3.41 us -> 5.21 us
    pallas_call x1, Pallas kernels: 155 us -> 140 us  [exchange(): pl.pallas_call(kernel, name='window', out_shape=(jax.ShapeDtypeStruct((DO...]
    mul x1 -> x0, other arithmetic: 3.4 us -> none  [local(): return (doc_share, word_weight * word_sum, topic_mean[0])]
    unnamed x8 -> x7, local copies, waits for them, and re-layouts: 1.94 us -> 5.21 us
where the time goes in v2:
time: 146 us
  Pallas kernels  140 us (96%)
  local copies, waits for them, and re-layouts  5.21 us (4%)
    pallas_call x1, Pallas kernels, exchange(): pl.pallas_call(kernel, name='window', out_shape=(jax.ShapeDtypeStruct((DO...  140 us
    unnamed x7, local copies, waits for them, and re-layouts  5.21 us

profile of v2, /device:TPU:1, one launch (start us, length us, event | category | flops | bytes accessed | tf_op | source)
XLA Modules:
  0.0 145.8 jit_solution(1610151987492558199)
XLA Ops:
  0.6 139.9 %window.1 = (bf16[256,4096]{1,0:T(8,128)(2,1)}, f32[128,4096]{1,0:T(8,128)}, f32[1,4096]{1,0:T(1,128)}) custom-call(s32[256,1024]{1,0:T(8,128)} %counts_in.1, s32[2,8]{1,0:T(2,128)} %live.1, s32[1,256]{1,0:T(1,128)} %bitcast.5, bf16[256,4096]{1,0:T(8,128)(2,1)} %mix_in.1, f32[128,4096]{1,0:T(8,128)} %topic_in.1, f32[1,4096]{1,0:T(1,128)} %bitcast.3), custom_call_target="tpu_custom_call" | custom-call | tf_op jit(solution)/shard_map/window/pallas_call | solution.py:649
  140.6 0.0 copy-start
  140.6 3.3 %copy.12 = bf16[256,4096]{1,0:T(8,128)(2,1)} copy(bf16[256,4096]{1,0:T(8,128)(2,1)} %get-tuple-element.12) | data formatting | bytes 4194304
  143.9 0.0 copy-done
  143.9 0.0 copy-start.1
  143.9 1.3 copy.13
  145.2 0.0 copy-done.1
  145.2 0.6 copy.14
Async XLA Ops:
  140.6 3.3 %copy-start = (f32[128,4096]{1,0:T(8,128)S(1)}, f32[128,4096]{1,0:T(8,128)}, u32[]{:S(2)}) copy-start(f32[128,4096]{1,0:T(8,128)} %get-tuple-element.13) | copy-start | bytes 6291460
  143.9 1.3 copy-start.1

commit v3 on v2

--- a/solution.py
+++ b/solution.py
@@ -43,7 +43,6 @@
     counts,
     mix,
     topic,
-    share,
     inverse,
     span,
     words,
@@ -84,7 +83,6 @@
     recv_tx,
     recv_tp,
     load,
-    store,
 ):
     grp = lax.axis_index("grp")
     blk = lax.axis_index("blk")
@@ -127,8 +125,8 @@
 
     mix_load = pltpu.make_async_copy(mix_in, mix, load.at[CH])
     counts_load = pltpu.make_async_copy(counts_in, counts, load.at[CH + 1])
-    for r in range(CH):
-        topic_load(r).start()
+    for u in range(CH):
+        topic_load(lax.rem(u + 2 * h, CH)).start()
     mix_load.start()
     counts_load.start()
 
@@ -168,9 +166,20 @@
 
     def to_y(j, r):
         slot = 4 * j + i
-        side = jnp.where(r < CH // 2, h, 1 - h)
-        return remote(
-            chunk(slot, r), chunk(slot, r), send_w.at[j, r, 2], recv_w.at[slot, r], h_=side, a_=1 - a
+        return remote(
+            chunk(slot, r), chunk(slot, r), send_w.at[j, r, 2], recv_w.at[slot, r], h_=lax.rem(r + h, 2), a_=1 - a
+        )
+
+    def to_other_y(r):
+        slot = 8 + i
+        return remote(
+            chunk(slot, r), chunk(slot, r), send_w.at[2, r, 4], recv_w.at[slot, r], h_=lax.rem(r + h + 1, 2), a_=1 - a
+        )
+
+    def to_far(r):
+        slot = 8 + i
+        return remote(
+            chunk(slot, r), chunk(slot, r), send_w.at[2, r, 0], recv_w.at[slot, r], h_=1 - h, c_=1 - c
         )
 
     def relay(j, r):
@@ -179,14 +188,25 @@
 
     def arrived(slot, r):
         return pltpu.make_async_copy(chunk(slot, r), chunk(slot, r), recv_w.at[slot, r])
+
+    def mine(r):
+        return lax.div(r, CH // 2) == h
 
     def column_copies(j, r, act):
         if j == 0:
             act(to_z(j, r))
         elif j == 1:
-            @pl.when(i <= 2)
+            @pl.when(jnp.logical_and(i <= 2, mine(r)))
             def _():
                 act(to_z(j, r))
+        else:
+            @pl.when(c == 0)
+            def _():
+                act(to_far(r))
+
+            @pl.when(a == 0)
+            def _():
+                act(to_other_y(r))
         if j == 1:
             act(to_partner(j, r))
             act(to_y(j, r))
@@ -205,8 +225,12 @@
     inverse[...] = 1.0 / (total[...] + beta_prior * VOCAB)
     span[...] = jnp.broadcast_to(lengths[...].astype(F32), (8, DOCS)).T[:, :1]
 
+    def turn(u):
+        return lax.rem(u + 2 * h, CH)
+
     @pl.loop(0, CH)
-    def _(r):
+    def _(u):
+        r = turn(u)
         rows = pl.ds(pl.multiple_of(r * ROWS, ROWS), ROWS)
         own = pl.ds(pl.multiple_of(i * WB + r * ROWS, ROWS), ROWS)
         topic_load(r).wait()
@@ -214,13 +238,13 @@
         topic[rows, :] = weight
         words[own, :] = weight.astype(BF16)
 
-        @pl.when(r == 0)
+        @pl.when(u == 0)
         def _():
             pl.semaphore_wait(barrier, greeted)
 
-        @pl.when(r > 0)
-        def _():
-            column_copies(0, r - 1, start)
+        @pl.when(u > 0)
+        def _():
+            column_copies(0, turn(u - 1), start)
 
     own_docs = 2 * x + c
     mix_load.wait()
@@ -235,7 +259,7 @@
 
         @pl.when(n == 0)
         def _():
-            column_copies(0, CH - 1, start)
+            column_copies(0, turn(CH - 1), start)
 
     def doc_rows(q):
         return pl.ds(pl.multiple_of(q * DOCS, DOCS), DOCS)
@@ -354,33 +378,35 @@
     def _(t):
         @pl.when(t <= 4)
         def _():
-            r = t - 1
+            r = turn(t - 1)
             arrived(4 + i, r).wait()
             column_copies(1, r, start)
 
         @pl.when(jnp.logical_and(t == 2, a == 0))
         def _():
-            for r in range(CH):
+            for u in range(CH):
+                r = lax.rem(2 * h + CH - u, CH)
                 arrived(i2, r).wait()
                 relay(0, r).start()
 
         @pl.when(jnp.logical_and(t >= 2, t <= 5))
         def _():
-            r = t - 2
+            r = lax.rem(2 * h + CH + 2 - t, CH)
             arrived(4 + i2, r).wait()
             relay(1, r).start()
 
-        @pl.when(jnp.logical_and(jnp.logical_and(t >= 5, t <= 8), i <= 2))
-        def _():
-            r = t - 5
+        @pl.when(jnp.logical_and(jnp.logical_and(t >= 5, t <= 6), i <= 2))
+        def _():
+            r = 2 * h + t - 5
             arrived(8 + i, r).wait()
             column_copies(2, r, start)
 
-        @pl.when(jnp.logical_and(jnp.logical_and(t >= 6, t <= 9), a == 1))
-        def _():
-            r = t - 6
-            arrived(8 + i2, r).wait()
-            relay(2, r).start()
+        @pl.when(jnp.logical_and(jnp.logical_and(t >= 6, t <= 7), a == 1))
+        def _():
+            for u in range(2):
+                r = t - 6 + 2 * u
+                arrived(8 + i2, r).wait()
+                relay(2, r).start()
 
         back = t - 3 - i
 
@@ -420,10 +446,7 @@
         weight = mix[:, at].astype(F32) * scale[...] + alpha_prior
         new = weight * proj
         column[:, at] = jnp.sum(new, axis=0, keepdims=True)
-        share[:, at] = (K * (new + alpha_prior) * under).astype(BF16)
-
-    share_store = pltpu.make_async_copy(share, share_out, store.at[2])
-    share_store.start()
+        share_out[:, at] = (K * (new + alpha_prior) * under).astype(BF16)
 
     def topic_z(dz):
         return remote(column, col_z.at[z], send_t.at[0, dz], recv_tz.at[z], z_=zo(dz))
@@ -569,24 +592,20 @@
         column_p += col_p[q]
     mean[...] = column_p * (1.0 / (WB * 32))
 
-    def topic_store(p):
-        return pltpu.make_async_copy(gathered.at[part_rows(p), :], topic_out.at[part_rows(p), :], store.at[p])
-
     for p in range(PARTS):
         rows = part_rows(p)
         for dx, dh, dc in fan:
             q = 2 * xo(dx) + co(dc)
             at = gathered.at[rows, piece(q, ho(dh))]
             pltpu.make_async_copy(at, at, recv_g.at[p, q, ho(dh)]).wait()
-        gathered[rows, :] = gathered[rows, :] * topic[rows, :]
-        topic_store(p).start()
+        topic_out[rows, :] = gathered[rows, :] * topic[rows, :]
 
     @pl.loop(0, CH)
     def _(r):
         column_copies(0, r, drain)
         column_copies(1, r, drain)
 
-        @pl.when(i <= 2)
+        @pl.when(jnp.logical_and(i <= 2, mine(r)))
         def _():
             column_copies(2, r, drain)
 
@@ -636,9 +655,6 @@
         drain(topic_x(dx))
     for where in plane:
         drain(topic_p(*where))
-    share_store.wait()
-    for p in range(PARTS):
-        topic_store(p).wait()
 
 
 def exchange(counts, tile_live, lengths, doc_mix, word_topic, topic_total):
@@ -650,17 +666,16 @@
         kernel,
         name="window",
         out_shape=(
-            jax.ShapeDtypeStruct((DOCS, K), BF16),
-            jax.ShapeDtypeStruct((WB, K), F32),
+            pltpu.VMEM((DOCS, K), BF16),
+            pltpu.VMEM((WB, K), F32),
             jax.ShapeDtypeStruct((1, K), F32),
         ),
         in_specs=[hbm, smem, vmem, hbm, hbm, vmem],
-        out_specs=(hbm, hbm, vmem),
+        out_specs=(vmem, vmem, vmem),
         scratch_shapes=[
             pltpu.VMEM((DOCS, SPAN * WB), jnp.int32),
             pltpu.VMEM((DOCS, K), BF16),
             pltpu.VMEM((WB, K), F32),
-            pltpu.VMEM((DOCS, K), BF16),
             pltpu.VMEM((1, K), F32),
             pltpu.VMEM((DOCS, 1), F32),
             pltpu.VMEM((SLOTS * WB, K), BF16),
@@ -681,7 +696,7 @@
             pltpu.VMEM((8, 1, K), F32),
             pltpu.VMEM((4, 1, K), F32),
             pltpu.VMEM((8, 1, K), F32),
-            dma((3, CH, 4)),
+            dma((3, CH, 5)),
             dma((SLOTS, CH)),
             dma((4, 2)),
             dma((8,)),
@@ -701,10 +716,9 @@
             dma((4,)),
             dma((8,)),
             dma((CH + 2,)),
-            dma((PARTS + 1,)),
         ],
         compiler_params=pltpu.CompilerParams(
-            collective_id=0, has_side_effects=True, vmem_limit_bytes=60 * 1024 * 1024
+            collective_id=0, has_side_effects=True, vmem_limit_bytes=62820000
         ),
     )(counts, tile_live, lengths, doc_mix, word_topic, topic_total)
 

time: 146 us -> 145 us (level)
  local copies, waits for them, and re-layouts: 5.21 us -> 3.25 us
    unnamed x7 -> x5, local copies, waits for them, and re-layouts: 5.21 us -> 3.25 us
where the time goes in v3:
time: 145 us
  Pallas kernels  141 us (97%)
  local copies, waits for them, and re-layouts  3.25 us (2%)
    pallas_call x1, Pallas kernels, exchange(): pl.pallas_call(kernel, name='window', out_shape=(pltpu.VMEM((DOCS, K), BF...  141 us
    unnamed x5, local copies, waits for them, and re-layouts  3.25 us

profile of v3, /device:TPU:1, one launch (start us, length us, event | category | flops | bytes accessed | tf_op | source)
XLA Modules:
  0.0 144.6 jit_solution(2831761716064323587)
XLA Ops:
  0.6 140.7 %window.1 = (bf16[256,4096]{1,0:T(8,128)(2,1)S(1)}, f32[128,4096]{1,0:T(8,128)S(1)}, f32[1,4096]{1,0:T(1,128)}) custom-call(s32[256,1024]{1,0:T(8,128)} %counts_in.1, s32[2,8]{1,0:T(2,128)} %live.1, s32[1,256]{1,0:T(1,128)} %bitcast.5, bf16[256,4096]{1,0:T(8,128)(2,1)} %mix_in.1, f32[128,4096]{1,0:T(8,128)} %topic_in.1, f32[1,4096]{1,0:T(1,128)} %bitcast.3), custom_call_target="tpu_custom_call" | custom-call | tf_op jit(solution)/shard_map/window/pallas_call | solution.py:665
  141.4 1.3 copy.12
  142.7 0.0 copy-start
  142.7 1.3 copy.13
  144.0 0.0 copy-done
  144.0 0.6 copy.14
Async XLA Ops:
  142.7 1.3 copy-start

commit v4 on v3

--- a/solution.py
+++ b/solution.py
@@ -23,7 +23,7 @@
 ROWS = WB // CH
 KD = K // 8
 KH = KD // 2
-PARTS = 2
+PARTS = 4
 
 
 def place(x, h, z, a, c):
@@ -77,6 +77,7 @@
     send_z,
     recv_z,
     send_g,
+    send_p,
     recv_g,
     send_t,
     recv_tz,
@@ -371,10 +372,37 @@
         def _():
             far_copy(m).start()
 
+    def topic_z(dz):
+        return remote(column, col_z.at[z], send_t.at[0, dz], recv_tz.at[z], z_=zo(dz))
+
+    def own_results():
+        length = jnp.sum(wlen[...], axis=1, keepdims=True)
+        under = 1.0 / (length + K * alpha_prior)
+
+        @pl.loop(0, K // 512)
+        def _(n):
+            at = pl.ds(pl.multiple_of(n * 512, 512), 512)
+            proj = jnp.dot(
+                ratio[...],
+                words[pl.ds(pl.multiple_of(i * WB, WB), SPAN * WB), at],
+                preferred_element_type=F32,
+            )
+            weight = mix[:, at].astype(F32) * scale[...] + alpha_prior
+            new = weight * proj
+            column[:, at] = jnp.sum(new, axis=0, keepdims=True)
+            share_out[:, at] = (K * (new + alpha_prior) * under).astype(BF16)
+
+        col_z[z] = column[...]
+        for dz in range(1, 8):
+            topic_z(dz).start()
+
     counts_load.wait()
     meet(i)
 
-    @pl.loop(1, SLOTS + 4)
+    def slot_at(e):
+        return jnp.where(jnp.logical_and(e >= 4, e < 8), 4 + lax.rem(e + 2 * a, 4), e)
+
+    @pl.loop(1, 19)
     def _(t):
         @pl.when(t <= 4)
         def _():
@@ -389,71 +417,58 @@
                 arrived(i2, r).wait()
                 relay(0, r).start()
 
-        @pl.when(jnp.logical_and(t >= 2, t <= 5))
-        def _():
-            r = lax.rem(2 * h + CH + 2 - t, CH)
+        @pl.when(jnp.logical_and(jnp.logical_or(t == 7, t == 9), i <= 2))
+        def _():
+            r = 2 * h + lax.div(t - 7, 2)
+            arrived(8 + i, r).wait()
+            column_copies(2, r, start)
+
+        @pl.when(jnp.logical_or(jnp.logical_and(t >= 2, t <= 4), t == 7))
+        def _():
+            r = lax.rem(2 * h + CH + 2 - jnp.minimum(t, 5), CH)
             arrived(4 + i2, r).wait()
             relay(1, r).start()
 
-        @pl.when(jnp.logical_and(jnp.logical_and(t >= 5, t <= 6), i <= 2))
-        def _():
-            r = 2 * h + t - 5
-            arrived(8 + i, r).wait()
-            column_copies(2, r, start)
-
-        @pl.when(jnp.logical_and(jnp.logical_and(t >= 6, t <= 7), a == 1))
+        @pl.when(jnp.logical_or(t <= 10, t >= 15))
+        def _():
+            slot = slot_at(jnp.where(t <= 10, t - 3, t - 7))
+
+            @pl.when(jnp.logical_and(t >= 3, jnp.logical_and(slot >= i, slot < i + SPAN)))
+            def _():
+                relay_ratio(slot - i)
+
+        @pl.when(jnp.logical_or(t <= 11, t >= 16))
+        def _():
+            ready = slot_at(jnp.where(t <= 11, t - 4, t - 8)) - 2 * a
+
+            @pl.when(jnp.logical_and(t >= 4, jnp.logical_and(ready >= 0, ready <= SPAN)))
+            def _():
+                products(ready)
+
+        @pl.when(jnp.logical_and(jnp.logical_or(t == 10, t == 12), a == 1))
         def _():
             for u in range(2):
-                r = t - 6 + 2 * u
+                r = lax.div(t - 10, 2) + 2 * u
                 arrived(8 + i2, r).wait()
                 relay(2, r).start()
 
-        back = t - 3 - i
-
-        @pl.when(jnp.logical_and(back >= 0, back < SPAN))
-        def _():
-            relay_ratio(back)
-
-        ready = t - 4 - 2 * a
-
-        @pl.when(jnp.logical_and(ready >= 0, ready <= SPAN))
-        def _():
-            products(ready)
-
-        slot = t - 1
-        column_of = lax.rem(slot, 4)
-
-        @pl.when(jnp.logical_and(slot > i, slot < i + SPAN))
-        def _():
-            @pl.when(jnp.logical_and(column_of != i, column_of != i2))
+        @pl.when(jnp.logical_or(t <= 8, jnp.logical_and(t >= 12, t <= 14)))
+        def _():
+            slot = slot_at(jnp.where(t <= 8, t - 1, t - 4))
+            column_of = lax.rem(slot, 4)
+
+            @pl.when(jnp.logical_and(slot > i, slot < i + SPAN))
             def _():
-                for r in range(CH):
-                    arrived(slot, r).wait()
-
-            meet(slot)
-
-    length = jnp.sum(wlen[...], axis=1, keepdims=True)
-    under = 1.0 / (length + K * alpha_prior)
-
-    @pl.loop(0, K // 512)
-    def _(n):
-        at = pl.ds(pl.multiple_of(n * 512, 512), 512)
-        proj = jnp.dot(
-            ratio[...],
-            words[pl.ds(pl.multiple_of(i * WB, WB), SPAN * WB), at],
-            preferred_element_type=F32,
-        )
-        weight = mix[:, at].astype(F32) * scale[...] + alpha_prior
-        new = weight * proj
-        column[:, at] = jnp.sum(new, axis=0, keepdims=True)
-        share_out[:, at] = (K * (new + alpha_prior) * under).astype(BF16)
-
-    def topic_z(dz):
-        return remote(column, col_z.at[z], send_t.at[0, dz], recv_tz.at[z], z_=zo(dz))
-
-    col_z[z] = column[...]
-    for dz in range(1, 8):
-        topic_z(dz).start()
+                @pl.when(jnp.logical_and(column_of != i, column_of != i2))
+                def _():
+                    for r in range(CH):
+                        arrived(slot, r).wait()
+
+                meet(slot)
+
+        @pl.when(t == 14)
+        def _():
+            own_results()
 
     def wait_far(m):
         pltpu.make_async_copy(far.at[m], far.at[m], recv_f.at[m]).wait()
@@ -550,8 +565,23 @@
             c_=co(dc),
         )
 
-    fan = [(dx, dh, dc) for dx in (2, 1, 3, 0) for dh in range(2) for dc in range(2) if dx + dh + dc]
-    for p in range(PARTS):
+    def gather_arrived(p, q, h_):
+        at = gathered.at[part_rows(p), piece(q, h_)]
+        return pltpu.make_async_copy(at, at, recv_g.at[p, q, h_])
+
+    def pass_y(p, dx, dc):
+        q = 2 * xo(dx) + dc
+        at = gathered.at[part_rows(p), piece(q, h)]
+        return remote(at, at, send_p.at[p, dx - 1, dc], recv_g.at[p, q, h], h_=1 - h)
+
+    def pass_x(p, dx, dc):
+        q = 2 * x + dc
+        at = gathered.at[part_rows(p), piece(q, 1 - h)]
+        return remote(at, at, send_p.at[p, dx - 1, dc], recv_g.at[p, q, 1 - h], x_=xo(dx))
+
+    fan = [(0, 1, 0), (0, 1, 1), (2, 0, 0), (2, 0, 1), (1, 0, 0), (1, 0, 1), (3, 0, 0), (3, 0, 1), (0, 0, 1)]
+
+    def spread(p):
         rows = part_rows(p)
         for q in range(2):
             hop_arrived(1, q, p).wait()
@@ -559,6 +589,24 @@
         gathered[rows, piece(own_docs, h)] = acc[c, rows]
         for where in fan:
             gather_copy(p, *where).start()
+
+    def pass_on(p):
+        if p % 2 == 0:
+            for dx in (1, 3, 2):
+                for dc in range(2):
+                    gather_arrived(p, 2 * xo(dx) + dc, h).wait()
+                    pass_y(p, dx, dc).start()
+        else:
+            for dc in range(2):
+                gather_arrived(p, 2 * x + dc, 1 - h).wait()
+                for dx in (2, 1, 3):
+                    pass_x(p, dx, dc).start()
+
+    for p in range(PARTS):
+        spread(p)
+        if p:
+            pass_on(p - 1)
+    pass_on(PARTS - 1)
 
     for dx in range(1, 4):
         q = xo(dx)
@@ -594,10 +642,14 @@
 
     for p in range(PARTS):
         rows = part_rows(p)
-        for dx, dh, dc in fan:
-            q = 2 * xo(dx) + co(dc)
-            at = gathered.at[rows, piece(q, ho(dh))]
-            pltpu.make_async_copy(at, at, recv_g.at[p, q, ho(dh)]).wait()
+        gather_arrived(p, 2 * x + 1 - c, h).wait()
+        for dc in range(2):
+            if p % 2 == 0:
+                gather_arrived(p, 2 * x + dc, 1 - h).wait()
+            for dx in range(1, 4):
+                if p % 2 == 1:
+                    gather_arrived(p, 2 * xo(dx) + dc, h).wait()
+                gather_arrived(p, 2 * xo(dx) + dc, 1 - h).wait()
         topic_out[rows, :] = gathered[rows, :] * topic[rows, :]
 
     @pl.loop(0, CH)
@@ -649,6 +701,9 @@
             drain(hop_copy(1, q, p))
         for where in fan:
             drain(gather_copy(p, *where))
+        for dx in range(1, 4):
+            for dc in range(2):
+                drain((pass_x if p % 2 else pass_y)(p, dx, dc))
     for dz in range(1, 8):
         drain(topic_z(dz))
     for dx in range(1, 4):
@@ -710,6 +765,7 @@
             dma((2, 2, PARTS)),
             dma((2, 2, PARTS)),
             dma((PARTS, 4, 2, 2)),
+            dma((PARTS, 3, 2)),
             dma((PARTS, 8, 2)),
             dma((3, 8)),
             dma((8,)),

time: 145 us -> 144 us (level)
  no operation moved by 1% of the time
where the time goes in v4:
time: 144 us
  Pallas kernels  140 us (97%)
  local copies, waits for them, and re-layouts  3.25 us (2%)
    pallas_call x1, Pallas kernels, exchange(): pl.pallas_call(kernel, name='window', out_shape=(pltpu.VMEM((DOCS, K), BF...  140 us
    unnamed x5, local copies, waits for them, and re-layouts  3.25 us

profile of v4, /device:TPU:1, one launch (start us, length us, event | category | flops | bytes accessed | tf_op | source)
XLA Modules:
  0.0 143.7 jit_solution(2992300275501937268)
XLA Ops:
  0.6 139.8 %window.1 = (bf16[256,4096]{1,0:T(8,128)(2,1)S(1)}, f32[128,4096]{1,0:T(8,128)S(1)}, f32[1,4096]{1,0:T(1,128)}) custom-call(s32[256,1024]{1,0:T(8,128)} %counts_in.1, s32[2,8]{1,0:T(2,128)} %live.1, s32[1,256]{1,0:T(1,128)} %bitcast.5, bf16[256,4096]{1,0:T(8,128)(2,1)} %mix_in.1, f32[128,4096]{1,0:T(8,128)} %topic_in.1, f32[1,4096]{1,0:T(1,128)} %bitcast.3), custom_call_target="tpu_custom_call" | custom-call | tf_op jit(solution)/shard_map/window/pallas_call | solution.py:720
  140.5 1.3 copy.12
  141.8 0.0 copy-start
  141.8 1.3 copy.13
  143.1 0.0 copy-done
  143.1 0.6 copy.14
Async XLA Ops:
  141.8 1.3 copy-start

commit v5 on v4

--- a/solution.py
+++ b/solution.py
@@ -24,6 +24,17 @@
 KD = K // 8
 KH = KD // 2
 PARTS = 4
+
+
+RELAYS = ({8: 0, 9: 2, 10: 4, 11: 6, 15: 8, 16: 9, 17: 10}, {8: 1, 9: 3, 10: 5, 11: 7})
+PRODUCTS = ({9: 0, 10: 2, 11: 4, 13: 6, 16: 8, 17: 9, 18: 10}, {9: 1, 10: 3, 11: 5, 14: 7})
+
+
+def pick(t, table):
+    e = jnp.int32(-1)
+    for step, place_ in table.items():
+        e = jnp.where(t == step, place_, e)
+    return e
 
 
 def place(x, h, z, a, c):
@@ -280,10 +291,6 @@
         )
 
     others = [(dx, dc) for dx in range(4) for dc in range(2) if dx + dc]
-    docs[doc_rows(own_docs), :] = doc_low[:, topics(own_docs)]
-    for dx, dc in others:
-        doc_copy(dx, dc).start()
-
     wlen[...] = jnp.zeros_like(wlen)
     for q in range(4):
         ratio_t[SPAN, :, 2 * q * DOCS : (2 * q + 1) * DOCS] = jnp.zeros((WB, DOCS), BF16)
@@ -398,6 +405,9 @@
 
     counts_load.wait()
     meet(i)
+    docs[doc_rows(own_docs), :] = doc_low[:, topics(own_docs)]
+    for dx, dc in others:
+        doc_copy(dx, dc).start()
 
     def slot_at(e):
         return jnp.where(jnp.logical_and(e >= 4, e < 8), 4 + lax.rem(e + 2 * a, 4), e)
@@ -428,22 +438,6 @@
             r = lax.rem(2 * h + CH + 2 - jnp.minimum(t, 5), CH)
             arrived(4 + i2, r).wait()
             relay(1, r).start()
-
-        @pl.when(jnp.logical_or(t <= 10, t >= 15))
-        def _():
-            slot = slot_at(jnp.where(t <= 10, t - 3, t - 7))
-
-            @pl.when(jnp.logical_and(t >= 3, jnp.logical_and(slot >= i, slot < i + SPAN)))
-            def _():
-                relay_ratio(slot - i)
-
-        @pl.when(jnp.logical_or(t <= 11, t >= 16))
-        def _():
-            ready = slot_at(jnp.where(t <= 11, t - 4, t - 8)) - 2 * a
-
-            @pl.when(jnp.logical_and(t >= 4, jnp.logical_and(ready >= 0, ready <= SPAN)))
-            def _():
-                products(ready)
 
         @pl.when(jnp.logical_and(jnp.logical_or(t == 10, t == 12), a == 1))
         def _():
@@ -466,6 +460,22 @@
 
                 meet(slot)
 
+        for table in PRODUCTS:
+            e = pick(t, table)
+            ready = slot_at(e) - 2 * a
+
+            @pl.when(jnp.logical_and(e >= 0, jnp.logical_and(ready >= 0, ready <= SPAN)))
+            def _():
+                products(ready)
+
+        for table in RELAYS:
+            e = pick(t, table)
+            slot = slot_at(e)
+
+            @pl.when(jnp.logical_and(e >= 0, jnp.logical_and(slot >= i, slot < i + SPAN)))
+            def _():
+                relay_ratio(slot - i)
+
         @pl.when(t == 14)
         def _():
             own_results()
@@ -493,6 +503,15 @@
     def hop_arrived(stage, q, p):
         at = (hop1, hop2)[stage].at[q, part_rows(p), :]
         return pltpu.make_async_copy(at, at, recv_z.at[stage, q, p])
+
+    for q in (0, 1):
+        wait_far(q)
+        acc[q] = part[q, h] + far[q]
+
+        @pl.when(a == 1)
+        def _():
+            wait_near(q)
+            acc[q] += near[0, q] + near[1, q]
 
     wait_far(4)
     acc[4] = part[8, h] + far[4]
@@ -515,15 +534,6 @@
         m = q - 2 + 2 * a
         wait_near(m)
         acc[q] += near[0, m] + near[1, m]
-    for q in (0, 1):
-        wait_far(q)
-        acc[q] = part[q, h] + far[q]
-
-        @pl.when(a == 1)
-        def _():
-            wait_near(q)
-            acc[q] += near[0, q] + near[1, q]
-
     for p in range(PARTS):
         rows = part_rows(p)
         hop_arrived(0, 0, p).wait()

time: 144 us -> 133 us (0.924)
  Pallas kernels: 140 us -> 129 us
    pallas_call x1, Pallas kernels: 140 us -> 129 us  [exchange(): pl.pallas_call(kernel, name='window', out_shape=(pltpu.VMEM((DOCS, K), BF...]
where the time goes in v5:
time: 133 us
  Pallas kernels  129 us (97%)
  local copies, waits for them, and re-layouts  3.25 us (2%)
    pallas_call x1, Pallas kernels, exchange(): pl.pallas_call(kernel, name='window', out_shape=(pltpu.VMEM((DOCS, K), BF...  129 us
    unnamed x5, local copies, waits for them, and re-layouts  3.25 us

profile of v5, /device:TPU:1, one launch (start us, length us, event | category | flops | bytes accessed | tf_op | source)
XLA Modules:
  0.0 132.7 jit_solution(17015582695817461682)
XLA Ops:
  0.6 128.8 %window.1 = (bf16[256,4096]{1,0:T(8,128)(2,1)S(1)}, f32[128,4096]{1,0:T(8,128)S(1)}, f32[1,4096]{1,0:T(1,128)}) custom-call(s32[256,1024]{1,0:T(8,128)} %counts_in.1, s32[2,8]{1,0:T(2,128)} %live.1, s32[1,256]{1,0:T(1,128)} %bitcast.5, bf16[256,4096]{1,0:T(8,128)(2,1)} %mix_in.1, f32[128,4096]{1,0:T(8,128)} %topic_in.1, f32[1,4096]{1,0:T(1,128)} %bitcast.3), custom_call_target="tpu_custom_call" | custom-call | tf_op jit(solution)/shard_map/window/pallas_call | solution.py:730
  129.4 1.3 copy.12
  130.8 0.0 copy-start
  130.8 1.3 copy.13
  132.1 0.0 copy-done
  132.1 0.6 copy.14
Async XLA Ops:
  130.8 1.3 copy-start

commit v6 on v5

--- a/solution.py
+++ b/solution.py
@@ -341,15 +341,25 @@
             ratio_arrived(2 * xo(dx) + c, k).wait()
             ratio_relay(k, dx).start()
 
-    def near_copy(m, side):
+    def half_rows(w):
+        return slice(w * WB // 2, (w + 1) * WB // 2)
+
+    def near_copy(m, side, w):
         n = m + 2 + 2 * lax.div(m, 2)
         return remote(
-            part.at[n, side], near.at[h, m], send_n.at[m, side], recv_n.at[h, m], h_=side, a_=1 - a
-        )
-
-    def far_copy(m):
+            part.at[n, side, half_rows(w), :],
+            near.at[h, m, half_rows(w), :],
+            send_n.at[m, side, w],
+            recv_n.at[h, m, w],
+            h_=side,
+            a_=1 - a,
+        )
+
+    def far_copy(m, w):
         n = m + 2 * lax.div(m, 2)
-        return remote(part.at[n, 1 - h], far.at[m], send_f.at[m], recv_f.at[m], h_=1 - h)
+        return remote(
+            part.at[n, 1 - h, half_rows(w), :], far.at[m, half_rows(w), :], send_f.at[m, w], recv_f.at[m, w], h_=1 - h
+        )
 
     def products(n):
         @pl.when(n == 0)
@@ -373,11 +383,11 @@
         @pl.when(lax.rem(lax.div(n, 2), 2) == 1)
         def _():
             for side in range(2):
-                near_copy(m - 2, side).start()
+                near_copy(m - 2, side, 0).start()
 
         @pl.when(lax.rem(lax.div(n, 2), 2) == 0)
         def _():
-            far_copy(m).start()
+            far_copy(m, 0).start()
 
     def topic_z(dz):
         return remote(column, col_z.at[z], send_t.at[0, dz], recv_tz.at[z], z_=zo(dz))
@@ -480,12 +490,23 @@
         def _():
             own_results()
 
-    def wait_far(m):
-        pltpu.make_async_copy(far.at[m], far.at[m], recv_f.at[m]).wait()
-
-    def wait_near(m):
+    @pl.loop(0, 4)
+    def _(m):
         for side in range(2):
-            pltpu.make_async_copy(near.at[side, m], near.at[side, m], recv_n.at[side, m]).wait()
+            near_copy(3 - m, side, 1).start()
+
+    @pl.loop(0, 5)
+    def _(m):
+        far_copy(4 - m, 1).start()
+
+    def wait_far(m, w):
+        at = far.at[m, half_rows(w), :]
+        pltpu.make_async_copy(at, at, recv_f.at[m, w]).wait()
+
+    def wait_near(m, w):
+        for side in range(2):
+            at = near.at[side, m, half_rows(w), :]
+            pltpu.make_async_copy(at, at, recv_n.at[side, m, w]).wait()
 
     def part_rows(p):
         return slice(p * WB // PARTS, (p + 1) * WB // PARTS)
@@ -504,37 +525,39 @@
         at = (hop1, hop2)[stage].at[q, part_rows(p), :]
         return pltpu.make_async_copy(at, at, recv_z.at[stage, q, p])
 
-    for q in (0, 1):
-        wait_far(q)
-        acc[q] = part[q, h] + far[q]
-
-        @pl.when(a == 1)
-        def _():
-            wait_near(q)
-            acc[q] += near[0, q] + near[1, q]
-
-    wait_far(4)
-    acc[4] = part[8, h] + far[4]
-
-    @pl.when(a == 0)
-    def _():
-        for q in (4, 5):
-            wait_near(q - 2)
-        acc[4] += near[0, 2] + near[1, 2]
-        acc[5] = near[0, 3] + near[1, 3]
-        for p in range(PARTS):
-            hop_copy(0, 1, p).start()
-
-    for p in range(PARTS):
-        hop_copy(0, 0, p).start()
-
-    for q in (2, 3):
-        wait_far(q)
-        acc[q] = part[(4, 5)[q - 2], h] + far[q]
-        m = q - 2 + 2 * a
-        wait_near(m)
-        acc[q] += near[0, m] + near[1, m]
-    for p in range(PARTS):
+    def sums_over_y(w):
+        rows = half_rows(w)
+        parts = range(w * PARTS // 2, (w + 1) * PARTS // 2)
+        for q in (0, 1):
+            wait_far(q, w)
+            acc[q, rows] = part[q, h, rows] + far[q, rows]
+
+            @pl.when(a == 1)
+            def _():
+                wait_near(q, w)
+                acc[q, rows] += near[0, q, rows] + near[1, q, rows]
+
+        wait_far(4, w)
+        acc[4, rows] = part[8, h, rows] + far[4, rows]
+
+        @pl.when(a == 0)
+        def _():
+            for m in (2, 3):
+                wait_near(m, w)
+            acc[4, rows] += near[0, 2, rows] + near[1, 2, rows]
+            acc[5, rows] = near[0, 3, rows] + near[1, 3, rows]
+            for p in parts:
+                hop_copy(0, 1, p).start()
+
+        for p in parts:
+            hop_copy(0, 0, p).start()
+        for q in (2, 3):
+            wait_far(q, w)
+            m = q - 2 + 2 * a
+            wait_near(m, w)
+            acc[q, rows] = part[(4, 5)[q - 2], h, rows] + far[q, rows] + near[0, m, rows] + near[1, m, rows]
+
+    def hop_on(p):
         rows = part_rows(p)
         hop_arrived(0, 0, p).wait()
         acc[2, rows] += hop1[0, rows]
@@ -546,6 +569,11 @@
 
         for q in range(2):
             hop_copy(1, q, p).start()
+
+    first, second = range(PARTS // 2), range(PARTS // 2, PARTS)
+    sums_over_y(0)
+    for p in first:
+        hop_on(p)
 
     for dz in range(1, 8):
         q = zo(dz)
@@ -612,11 +640,18 @@
                 for dx in (2, 1, 3):
                     pass_x(p, dx, dc).start()
 
-    for p in range(PARTS):
+    for p in first:
         spread(p)
-        if p:
-            pass_on(p - 1)
-    pass_on(PARTS - 1)
+    sums_over_y(1)
+    pass_on(0)
+    for p in second:
+        hop_on(p)
+    for p in first[1:]:
+        pass_on(p)
+    for p in second:
+        spread(p)
+    for p in second:
+        pass_on(p)
 
     for dx in range(1, 4):
         q = xo(dx)
@@ -694,11 +729,13 @@
     @pl.loop(0, 4)
     def _(m):
         for side in range(2):
-            drain(near_copy(m, side))
+            for w in range(2):
+                drain(near_copy(m, side, w))
 
     @pl.loop(0, 5)
     def _(m):
-        drain(far_copy(m))
+        for w in range(2):
+            drain(far_copy(m, w))
 
     for p in range(PARTS):
         drain(hop_copy(0, 0, p))
@@ -768,10 +805,10 @@
             dma((SPAN, 4)),
             dma((SPAN, 3)),
             dma((8, SPAN)),
-            dma((4, 2)),
-            dma((2, 4)),
-            dma((5,)),
-            dma((5,)),
+            dma((4, 2, 2)),
+            dma((2, 4, 2)),
+            dma((5, 2)),
+            dma((5, 2)),
             dma((2, 2, PARTS)),
             dma((2, 2, PARTS)),
             dma((PARTS, 4, 2, 2)),

time: 133 us -> 128 us (0.962)
  Pallas kernels: 129 us -> 124 us
    pallas_call x1, Pallas kernels: 129 us -> 124 us  [exchange(): pl.pallas_call(kernel, name='window', out_shape=(pltpu.VMEM((DOCS, K), BF...]
where the time goes in v6:
time: 128 us
  Pallas kernels  124 us (97%)
  local copies, waits for them, and re-layouts  3.25 us (3%)
    pallas_call x1, Pallas kernels, exchange(): pl.pallas_call(kernel, name='window', out_shape=(pltpu.VMEM((DOCS, K), BF...  124 us
    unnamed x5, local copies, waits for them, and re-layouts  3.25 us

profile of v6, /device:TPU:1, one launch (start us, length us, event | category | flops | bytes accessed | tf_op | source)
XLA Modules:
  0.0 127.9 jit_solution(2538879732611545224)
XLA Ops:
  0.6 124.0 %window.1 = (bf16[256,4096]{1,0:T(8,128)(2,1)S(1)}, f32[128,4096]{1,0:T(8,128)S(1)}, f32[1,4096]{1,0:T(1,128)}) custom-call(s32[256,1024]{1,0:T(8,128)} %counts_in.1, s32[2,8]{1,0:T(2,128)} %live.1, s32[1,256]{1,0:T(1,128)} %bitcast.5, bf16[256,4096]{1,0:T(8,128)(2,1)} %mix_in.1, f32[128,4096]{1,0:T(8,128)} %topic_in.1, f32[1,4096]{1,0:T(1,128)} %bitcast.3), custom_call_target="tpu_custom_call" | custom-call | tf_op jit(solution)/shard_map/window/pallas_call | solution.py:767
  124.6 1.3 %copy.12 = bf16[256,4096]{1,0:T(8,128)(2,1)} copy(bf16[256,4096]{1,0:T(8,128)(2,1)S(1)} %get-tuple-element.9) | data formatting | bytes 4194304
  126.0 0.0 copy-start
  126.0 1.3 %copy.13 = f32[128,4096]{1,0:T(8,128)} copy(f32[128,4096]{1,0:T(8,128)S(1)} %get-tuple-element.10) | data formatting | bytes 4194304
  127.3 0.0 copy-done
  127.3 0.6 copy.14
Async XLA Ops:
  126.0 1.3 %copy-start = (f32[1,4096]{1,0:T(1,128)S(1)}, f32[1,4096]{1,0:T(1,128)}, u32[]{:S(2)}) copy-start(f32[1,4096]{1,0:T(1,128)} %get-tuple-element.8) | copy-start | bytes 49156

commit v7 on v6

--- a/solution.py
+++ b/solution.py
@@ -168,6 +168,9 @@
     def chunk(slot, r):
         return words.at[pl.ds(pl.multiple_of(slot * WB + r * ROWS, ROWS), ROWS), :]
 
+    def turn(u):
+        return lax.rem(u + 2 * h, CH)
+
     def to_z(j, r):
         slot = 4 * j + i
         return remote(chunk(slot, r), chunk(slot + 4, r), send_w.at[j, r, 0], recv_w.at[slot + 4, r], z_=zo(-1))
@@ -201,13 +204,23 @@
     def arrived(slot, r):
         return pltpu.make_async_copy(chunk(slot, r), chunk(slot, r), recv_w.at[slot, r])
 
+    def swap(r):
+        slot = 4 + i
+        return remote(chunk(slot, r), chunk(slot, r), send_w.at[1, r, 4], recv_w.at[slot, r], h_=1 - h)
+
     def mine(r):
         return lax.div(r, CH // 2) == h
 
     def column_copies(j, r, act):
         if j == 0:
-            act(to_z(j, r))
+            @pl.when(r != turn(CH - 1))
+            def _():
+                act(to_z(j, r))
         elif j == 1:
+            @pl.when(r == turn(1))
+            def _():
+                act(swap(r))
+
             @pl.when(jnp.logical_and(i <= 2, mine(r)))
             def _():
                 act(to_z(j, r))
@@ -236,9 +249,6 @@
 
     inverse[...] = 1.0 / (total[...] + beta_prior * VOCAB)
     span[...] = jnp.broadcast_to(lengths[...].astype(F32), (8, DOCS)).T[:, :1]
-
-    def turn(u):
-        return lax.rem(u + 2 * h, CH)
 
     @pl.loop(0, CH)
     def _(u):

time: 128 us -> 131 us (1.023)
  Pallas kernels: 124 us -> 127 us
    pallas_call x1, Pallas kernels: 124 us -> 127 us  [exchange(): pl.pallas_call(kernel, name='window', out_shape=(pltpu.VMEM((DOCS, K), BF...]
where the time goes in v7:
time: 131 us
  Pallas kernels  127 us (97%)
  local copies, waits for them, and re-layouts  3.25 us (2%)
    pallas_call x1, Pallas kernels, exchange(): pl.pallas_call(kernel, name='window', out_shape=(pltpu.VMEM((DOCS, K), BF...  127 us
    unnamed x5, local copies, waits for them, and re-layouts  3.25 us

profile of v7, /device:TPU:1, one launch (start us, length us, event | category | flops | bytes accessed | tf_op | source)
XLA Modules:
  0.0 130.8 jit_solution(8364888616623276224)
XLA Ops:
  0.6 126.9 %window.1 = (bf16[256,4096]{1,0:T(8,128)(2,1)S(1)}, f32[128,4096]{1,0:T(8,128)S(1)}, f32[1,4096]{1,0:T(1,128)}) custom-call(s32[256,1024]{1,0:T(8,128)} %counts_in.1, s32[2,8]{1,0:T(2,128)} %live.1, s32[1,256]{1,0:T(1,128)} %bitcast.5, bf16[256,4096]{1,0:T(8,128)(2,1)} %mix_in.1, f32[128,4096]{1,0:T(8,128)} %topic_in.1, f32[1,4096]{1,0:T(1,128)} %bitcast.3), custom_call_target="tpu_custom_call" | custom-call | tf_op jit(solution)/shard_map/window/pallas_call | solution.py:777
  127.6 1.3 %copy.12 = bf16[256,4096]{1,0:T(8,128)(2,1)} copy(bf16[256,4096]{1,0:T(8,128)(2,1)S(1)} %get-tuple-element.9) | data formatting | bytes 4194304
  128.9 0.0 copy-start
  128.9 1.3 %copy.13 = f32[128,4096]{1,0:T(8,128)} copy(f32[128,4096]{1,0:T(8,128)S(1)} %get-tuple-element.10) | data formatting | bytes 4194304
  130.2 0.0 copy-done
  130.2 0.6 copy.14
Async XLA Ops:
  128.9 1.3 %copy-start = (f32[1,4096]{1,0:T(1,128)S(1)}, f32[1,4096]{1,0:T(1,128)}, u32[]{:S(2)}) copy-start(f32[1,4096]{1,0:T(1,128)} %get-tuple-element.8) | copy-start | bytes 49156

commit v8 on v6

--- a/solution.py
+++ b/solution.py
@@ -259,6 +259,27 @@
             column_copies(0, turn(u - 1), start)
 
     own_docs = 2 * x + c
+
+    def doc_rows(q):
+        return pl.ds(pl.multiple_of(q * DOCS, DOCS), DOCS)
+
+    def topics(q):
+        return pl.ds(pl.multiple_of(q * KD, KD), KD)
+
+    def doc_copy(dx, dc, w):
+        to = 2 * xo(dx) + co(dc)
+        half = DOCS // 2
+        return remote(
+            doc_low.at[w * half : (w + 1) * half, topics(to)],
+            docs.at[pl.ds(pl.multiple_of(own_docs * DOCS + w * half, half), half), :],
+            send_d.at[dx, dc, w],
+            recv_d.at[own_docs, w],
+            x_=xo(dx),
+            c_=co(dc),
+        )
+
+    others = [(dx, dc) for dx in (2, 1, 3, 0) for dc in range(2) if dx + dc]
+
     mix_load.wait()
 
     @pl.loop(0, DOCS // 32)
@@ -273,24 +294,11 @@
         def _():
             column_copies(0, turn(CH - 1), start)
 
-    def doc_rows(q):
-        return pl.ds(pl.multiple_of(q * DOCS, DOCS), DOCS)
-
-    def topics(q):
-        return pl.ds(pl.multiple_of(q * KD, KD), KD)
-
-    def doc_copy(dx, dc):
-        to = 2 * xo(dx) + co(dc)
-        return remote(
-            doc_low.at[:, topics(to)],
-            docs.at[doc_rows(own_docs), :],
-            send_d.at[dx, dc],
-            recv_d.at[own_docs],
-            x_=xo(dx),
-            c_=co(dc),
-        )
-
-    others = [(dx, dc) for dx in range(4) for dc in range(2) if dx + dc]
+        @pl.when(n == DOCS // 64)
+        def _():
+            for dx, dc in others:
+                doc_copy(dx, dc, 0).start()
+
     wlen[...] = jnp.zeros_like(wlen)
     for q in range(4):
         ratio_t[SPAN, :, 2 * q * DOCS : (2 * q + 1) * DOCS] = jnp.zeros((WB, DOCS), BF16)
@@ -332,12 +340,12 @@
         ratio_t[k + c, :, doc_rows(own_docs)] = wide.T.astype(BF16)
         ratio[:, at] = wide.astype(BF16)
         wlen[...] += kept
-        for dx in range(1, 4):
+        for dx in (2, 1, 3):
             ratio_out(k, dx).start()
         ratio_over(k).start()
 
     def relay_ratio(k):
-        for dx in range(1, 4):
+        for dx in (1, 3, 2):
             ratio_arrived(2 * xo(dx) + c, k).wait()
             ratio_relay(k, dx).start()
 
@@ -366,7 +374,9 @@
         def _():
             for dx, dc in others:
                 q = 2 * xo(dx) + co(dc)
-                pltpu.make_async_copy(docs.at[doc_rows(q), :], docs.at[doc_rows(q), :], recv_d.at[q]).wait()
+                for w in range(2):
+                    at = docs.at[pl.ds(pl.multiple_of(q * DOCS + w * DOCS // 2, DOCS // 2), DOCS // 2), :]
+                    pltpu.make_async_copy(at, at, recv_d.at[q, w]).wait()
 
         k = n - (1 - c)
 
@@ -413,11 +423,11 @@
         for dz in range(1, 8):
             topic_z(dz).start()
 
+    for dx, dc in others:
+        doc_copy(dx, dc, 1).start()
     counts_load.wait()
     meet(i)
     docs[doc_rows(own_docs), :] = doc_low[:, topics(own_docs)]
-    for dx, dc in others:
-        doc_copy(dx, dc).start()
 
     def slot_at(e):
         return jnp.where(jnp.logical_and(e >= 4, e < 8), 4 + lax.rem(e + 2 * a, 4), e)
@@ -717,7 +727,8 @@
             drain(relay(2, r))
 
     for dx, dc in others:
-        drain(doc_copy(dx, dc))
+        for w in range(2):
+            drain(doc_copy(dx, dc, w))
 
     @pl.loop(0, SPAN)
     def _(k):
@@ -800,8 +811,8 @@
             pltpu.VMEM((8, 1, K), F32),
             dma((3, CH, 5)),
             dma((SLOTS, CH)),
-            dma((4, 2)),
-            dma((8,)),
+            dma((4, 2, 2)),
+            dma((8, 2)),
             dma((SPAN, 4)),
             dma((SPAN, 3)),
             dma((8, SPAN)),

time: 128 us -> 128 us (level)
  no operation moved by 1% of the time
where the time goes in v8:
time: 128 us
  Pallas kernels  124 us (97%)
  local copies, waits for them, and re-layouts  3.25 us (3%)
    pallas_call x1, Pallas kernels, exchange(): pl.pallas_call(kernel, name='window', out_shape=(pltpu.VMEM((DOCS, K), BF...  124 us
    unnamed x5, local copies, waits for them, and re-layouts  3.25 us

profile of v8, /device:TPU:1, one launch (start us, length us, event | category | flops | bytes accessed | tf_op | source)
XLA Modules:
  0.0 127.7 jit_solution(14964523349975689245)
XLA Ops:
  0.6 123.8 %window.1 = (bf16[256,4096]{1,0:T(8,128)(2,1)S(1)}, f32[128,4096]{1,0:T(8,128)S(1)}, f32[1,4096]{1,0:T(1,128)}) custom-call(s32[256,1024]{1,0:T(8,128)} %counts_in.1, s32[2,8]{1,0:T(2,128)} %live.1, s32[1,256]{1,0:T(1,128)} %bitcast.5, bf16[256,4096]{1,0:T(8,128)(2,1)} %mix_in.1, f32[128,4096]{1,0:T(8,128)} %topic_in.1, f32[1,4096]{1,0:T(1,128)} %bitcast.3), custom_call_target="tpu_custom_call" | custom-call | tf_op jit(solution)/shard_map/window/pallas_call | solution.py:778
  124.5 1.3 %copy.12 = bf16[256,4096]{1,0:T(8,128)(2,1)} copy(bf16[256,4096]{1,0:T(8,128)(2,1)S(1)} %get-tuple-element.9) | data formatting | bytes 4194304
  125.8 0.0 copy-start
  125.8 1.3 %copy.13 = f32[128,4096]{1,0:T(8,128)} copy(f32[128,4096]{1,0:T(8,128)S(1)} %get-tuple-element.10) | data formatting | bytes 4194304
  127.1 0.0 copy-done
  127.1 0.6 copy.14
Async XLA Ops:
  125.8 1.3 %copy-start = (f32[1,4096]{1,0:T(1,128)S(1)}, f32[1,4096]{1,0:T(1,128)}, u32[]{:S(2)}) copy-start(f32[1,4096]{1,0:T(1,128)} %get-tuple-element.8) | copy-start | bytes 49156
